TPU v7x, 512 devices: a whole 4x8x8 slice. The times are simulated.
512 devices in a mesh: cam: 16 (over x_lo, y), space: 32 (over x_hi, z, core).
Axes of the slice: x: 4 (x_hi: 2, x_lo: 2; x = x_hi * 2 + x_lo), y: 8, z: 8, core: 2. Of those that a mesh axis runs over, the one named last changes fastest.
Arguments:
- features: float32 [64, 131072], P(None, ('cam', 'space')), may hold values from -6 to 6
- positions: float32 [3, 131072], P(None, ('cam', 'space')), may hold values from -6144 to 6144, as said below
- spreads: float32 [131072], P(('cam', 'space')), may hold values from 16 to 64
- logits: float32 [131072], P(('cam', 'space')), may hold values from -6 to -2
- camera: float32 [16, 3], replicated, may hold values from -1 to 1
- decoder: bfloat16 [64, 512], replicated, may hold values from -0.75 to 0.75
- tile_lists: int32 [16, 32, 16, 256], P('cam', 'space'), may hold values from 0 to 8191, as said below
- counts: int32 [16, 32, 16], P('cam', 'space'), may hold values from 1 to 256, as said below
- targets: bfloat16 [16, 32, 16, 256, 512], P('cam', 'space'), may hold values from -6 to 6
Outputs:
- grad_features: float32 [64, 131072], P(None, ('cam', 'space'))
- grad_logits: float32 [131072], P(('cam', 'space'))
Inputs may be any that keep to these rules, and one draw needn't show every extreme that they name: `positions`: rows are x, y and depth; depth lies between 4 and 8. `tile_lists`: the list of tile (c, s, j) names only ids j * 256 + q or 4096 + j * 256 + q with 0 <= q < 256, no id twice; lists of tile row 0 name only ids below 4096. `counts`: some tile has all 256 entries live.
All inputs are finite; a program needn't handle non-finite values.
Results may differ from a plain program's by a relative error of at most 0.003.
Values may be sent and summed in bfloat16 or wider, within the bound.
No kernel may reach another device: no remote copies, remote signals or barrier semaphores. Data moves between devices by JAX's collectives and lax.ppermute only.
A program may use at most 64 MiB of HBM per device.

v0:
```python
import jax
import jax.numpy as jnp
from jax import lax
from jax.sharding import PartitionSpec as P

TS = 16


def shifted(shard, axis, by):
    length = lax.axis_size(axis)
    pairs = [(i, i + by) for i in range(length) if 0 <= i + by < length]
    return lax.ppermute(shard, axis, pairs)


def project_terms(
    gathered, viewers, tile_row, columns, live_counts, grad_maker, image_width, image_height
):
    channels = gathered.shape[0] - 5
    tiles_here = gathered.shape[1]
    length = gathered.shape[2]
    step_len = 128
    block_count = length // step_len
    pixel_count = TS * TS
    feature_bf = gathered[:channels].astype(jnp.bfloat16)
    distance = gathered[channels + 2] - 0.05 * viewers[:, 2:3]
    centre_u = (gathered[channels] - 0.75 * TS * viewers[:, 0:1]) / distance + 0.5 * image_width
    centre_v = (
        gathered[channels + 1] - 0.75 * TS * viewers[:, 1:2]
    ) / distance + 0.5 * image_height
    radius = gathered[channels + 3] / distance
    sigmoid_open = jax.nn.sigmoid(gathered[channels + 4])
    opacity = 0.99 * sigmoid_open
    sigmoid_slope = 0.99 * sigmoid_open * (1.0 - sigmoid_open)
    pixel_id = jnp.arange(pixel_count, dtype=jnp.int32)
    pixel_u = (columns[:, None] * TS + pixel_id[None, :] % TS).astype(jnp.float32) + 0.5
    pixel_v = (tile_row * TS + pixel_id // TS).astype(jnp.float32) + 0.5
    alive_mask = (jnp.arange(length, dtype=jnp.int32)[None, :] < live_counts[:, None]).astype(
        jnp.float32
    )
    logit_gate_all = alive_mask * sigmoid_slope
    steps_used = (jnp.max(live_counts) + step_len - 1) // step_len

    def block_terms(first_entry):

        def window_of(source_array):
            return lax.dynamic_slice_in_dim(
                source_array, first_entry, step_len, axis=source_array.ndim - 1
            )

        delta_u = pixel_u[:, :, None] - window_of(centre_u)[:, None, :]
        delta_v = pixel_v[None, :, None] - window_of(centre_v)[:, None, :]
        spread = window_of(radius)[:, None, :]
        falloff = jnp.exp(-(delta_u * delta_u + delta_v * delta_v) / (2.0 * spread * spread))
        opaque = (window_of(opacity) * window_of(alive_mask))[:, None, :] * falloff
        log_keep = jnp.log(1.0 - opaque)
        inner_log = jnp.cumsum(log_keep, axis=2) - log_keep
        return (
            falloff,
            opaque,
            log_keep,
            inner_log,
            window_of(feature_bf),
            window_of(logit_gate_all),
        )

    def forward(position, state_in):
        log_start, feature_sum, starts = state_in
        first_entry = position * step_len
        falloff, opaque, log_keep, inner_log, block_feat, unused = block_terms(first_entry)
        weight = opaque * jnp.exp(log_start[:, :, None] + inner_log)
        feature_sum = feature_sum + jnp.einsum(
            "tpk,ctk->tcp",
            weight.astype(jnp.bfloat16),
            block_feat,
            preferred_element_type=jnp.float32,
        )
        starts = lax.dynamic_update_index_in_dim(starts, log_start, position, 0)
        return (log_start + jnp.sum(log_keep, axis=2), feature_sum, starts)

    initial = (
        jnp.zeros((tiles_here, pixel_count), jnp.float32),
        jnp.zeros((tiles_here, channels, pixel_count), jnp.float32),
        jnp.zeros((block_count, tiles_here, pixel_count), jnp.float32),
    )
    unused_log, feature_sum, starts = lax.fori_loop(0, steps_used, forward, initial)
    composite = feature_sum.astype(jnp.bfloat16)
    pixel_grad = grad_maker(composite).astype(jnp.bfloat16)

    def backward(reverse_turn, state_in):
        behind_sum, feature_grad, logit_grad = state_in
        position = steps_used - 1 - reverse_turn
        first_entry = position * step_len
        falloff, opaque, log_keep, inner_log, block_feat, logit_gate = block_terms(first_entry)
        keep_to = jnp.exp(
            lax.dynamic_index_in_dim(starts, position, 0, keepdims=False)[:, :, None] + inner_log
        )
        weight = opaque * keep_to
        weight_bf = weight.astype(jnp.bfloat16)
        contrib = jnp.einsum(
            "tcp,ctk->tpk", pixel_grad, block_feat, preferred_element_type=jnp.float32
        )
        weighted = weight * contrib
        block_total = jnp.sum(weighted, axis=2)
        behind = behind_sum[:, :, None] + block_total[:, :, None] - jnp.cumsum(weighted, axis=2)
        dopaque = keep_to * contrib - behind / (1.0 - opaque)
        logit_part = logit_gate * jnp.sum(dopaque * falloff, axis=1)
        feature_part = jnp.einsum(
            "tpk,tcp->ctk", weight_bf, pixel_grad, preferred_element_type=jnp.float32
        )
        feature_grad = lax.dynamic_update_slice_in_dim(
            feature_grad, feature_part, first_entry, axis=2
        )
        logit_grad = lax.dynamic_update_slice_in_dim(logit_grad, logit_part, first_entry, axis=1)
        return (behind_sum + block_total, feature_grad, logit_grad)

    initial_back = (
        jnp.zeros((tiles_here, pixel_count), jnp.float32),
        jnp.zeros((channels, tiles_here, length), jnp.float32),
        jnp.zeros((tiles_here, length), jnp.float32),
    )
    unused_behind, feature_grad, logit_grad = lax.fori_loop(0, steps_used, backward, initial_back)
    return (feature_grad, logit_grad)


def full_target_rule(pixel_targets, decoder):
    decoder_wide = decoder.astype(jnp.float32)

    def make_grad(composite):
        decoded = jnp.einsum("tcp,cd->tpd", composite, decoder, preferred_element_type=jnp.float32)
        residual = decoded - pixel_targets.astype(jnp.float32)
        return jnp.einsum("tpd,cd->tcp", residual, decoder_wide, precision=lax.Precision.HIGHEST)

    return make_grad


def on_device(features, positions, spreads, logits, camera, decoder, tile_lists, counts, targets):
    channels = features.shape[0]
    length = features.shape[1]
    camera_count = lax.axis_size("cam")
    space_count = lax.axis_size("space")
    camera_id = lax.axis_index("cam")
    tile_row = lax.axis_index("space")
    image_width = TS * camera_count
    image_height = TS * space_count
    block_rows = camera_count * length
    own_slab = jnp.concatenate([features, positions, spreads[None], logits[None]], axis=0)
    upper_slab = shifted(own_slab, "space", 1)
    both_slabs = lax.all_gather(jnp.stack([own_slab, upper_slab]), "cam", axis=2, tiled=True)
    gauss_table = jnp.concatenate([both_slabs[0], both_slabs[1]], axis=1)
    entries = tile_lists[0, 0]
    picker = (jnp.arange(camera_count, dtype=jnp.int32) == camera_id).astype(jnp.float32)
    viewers = jnp.broadcast_to(jnp.sum(camera * picker[:, None], axis=0), (camera_count, 3))
    columns = jnp.arange(camera_count, dtype=jnp.int32)
    gathered = jnp.take(gauss_table, entries, axis=1)
    grad_maker = full_target_rule(targets[0, 0], decoder)
    feature_grad, logit_grad = project_terms(
        gathered, viewers, tile_row, columns, counts[0, 0], grad_maker, image_width, image_height
    )
    values = jnp.concatenate([feature_grad, logit_grad[None]], axis=0)
    totals = jnp.zeros((channels + 1, 2 * block_rows), jnp.float32).at[:, entries].add(values)
    returned = shifted(totals[:, block_rows:], "space", -1)
    summed = lax.psum_scatter(
        totals[:, :block_rows] + returned, "cam", scatter_dimension=1, tiled=True
    )
    return (summed[:channels], summed[channels])


def solution(mesh):
    placed = (
        P(None, ("cam", "space")),
        P(None, ("cam", "space")),
        P(("cam", "space")),
        P(("cam", "space")),
        P(),
        P(),
        P("cam", "space", None, None),
        P("cam", "space", None),
        P("cam", "space", None, None, None),
    )
    return jax.shard_map(
        on_device,
        mesh=mesh,
        in_specs=placed,
        out_specs=(P(None, ("cam", "space")), P(("cam", "space"))),
        check_vma=False,
    )
```

profile of v0, /device:TPU:4, one launch (start us, length us, event | category | flops | bytes accessed | tf_op | source)
XLA Modules:
  0.0 300.4 jit_solution(15788181093214662596)
XLA Ops:
  7.3 0.9 copy.57
  10.8 1.9 collective-permute-start
  12.9 10.9 %collective-permute-done = f32[69,256]{0,1:T(8,128)S(1)} collective-permute-done((f32[69,256]{0,1:T(8,128)S(1)}, f32[69,256]{0,1:T(8,128)S(1)}, u32[]{:S(2)}, u32[]{:S(2)}) %collective-permute-start) | collective-permute-done | bytes 70688 | tf_op jit(solution)/shard_map/ppermute | solution.py:12
  28.9 72.8 %all-gather.2.cloned.1.call-done = f32[2,69,4096]{1,2,0:T(8,128)} async-done(((f32[2,69,256]{1,2,0:T(8,128)}), f32[2,69,4096]{1,2,0:T(8,128)}) %all-gather.2.cloned.1.call-update) | async-done | bytes 2261008 | tf_op jit(solution)/shard_map/all_gather | solution.py:148
  101.7 2.5 slice_bitcast_fusion.1
  104.2 2.2 pad_maximum_fusion
  106.4 13.0 %gather_fusion = f32[4096,69]{1,0:T(8,128)S(1)} fusion(f32[69,8192]{0,1:T(8,128)} %pad_maximum_fusion, s32[4096]{0:T(1024)S(1)} %broadcast_clamp_fusion), kind=kCustom, calls=%fused_computation | custom fusion | bytes 2277376 | tf_op jit(solution)/shard_map/jit(_take)/gather | solution.py:154
  119.3 1.0 copy.61
  121.0 5.7 %while.32 = (s32[]{:T(128)}, f32[16,256]{1,0:T(8,128)S(1)}, f32[16,64,256]{2,1,0:T(8,128)S(1)}, f32[2,16,256]{2,1,0:T(8,128)S(1)}, s32[]{:T(128)}, /*index=5*/f3...) while((s32[]{:T(128)}, f32[16,256]{1,0:T(8,128)S(1)}, ...), condition=%wide.region_5.6_spmd.clone, body=%wide.region_2.5_spmd.clone.sunk | while | flops 150754048 | bytes 4895069 | solution.py:85
  121.7 1.5 fusion.84
  123.1 2.8 multiply_convert_fusion.2
  126.7 1.3 fusion.44
  128.0 0.9 copy-done.1
  128.9 4.9 %fusion.43 = bf16[16,64,256]{2,1,0:T(8,128)(2,1)S(1)} fusion(f32[16,256,512]{2,1,0:T(8,128)S(1)} %fusion.44, bf16[1,1,16,256,512]{4,3,2,1,0:T(8,128)(2,1)S(1)} %copy-done.1, bf16[64,512]{1,0:T(8,128)(2,1)S(1)} %copy-done), kind=kOutput, calls=%fused_computation.78 | convolution fusion | flops 1615069184 | bytes 13172736 | tf_op jit(solution)/shard_map/tpd,cd->tcp/dot_general | solution.py:131
  133.9 13.1 %while.33 = (s32[]{:T(128)}, f32[16,256]{1,0:T(8,128)S(1)}, f32[64,16,256]{2,0,1:T(8,128)S(1)}, f32[16,256]{1,0:T(8,128)S(1)}, s32[]{:T(128)}, /*index=5*/s32[]{...) while((s32[]{:T(128)}, f32[16,256]{1,0:T(8,128)S(1)}, ...), condition=%wide.region_11.12_spmd.clone, body=%wide.region_6.11_spmd.clone.sunk | while | flops 295195392 | bytes 27490700 | solution.py:121
  134.3 1.2 subtract_log_fusion.8
  135.4 1.3 fusion.91
  136.7 2.2 fusion.93
  138.9 2.5 fusion.92
  141.4 1.3 fusion.94
  142.7 4.2 %fusion.95 = f32[16,128]{1,0:T(8,128)S(1)} fusion(f32[16,128,256]{2,1,0:T(8,128)S(1)} %get-tuple-element.746, f32[16,256,128]{1,0,2:T(8,128)S(1)} %fusion.94, f32[16,256]{1,0:T(8,128)S(1)} %add.491, f32[16,128]{1,0:T(8,128)S(1)} %get-tuple-element.741, f32[16,128]{1,0:T(8,128)S(1)} %get-tuple-element.742, f32[256]{0:T(256)S(1)} %fusion.90, ...), kind=kLoop, calls=%fused_computation.35.clone.1 | loop fusion | flops 8910848 | bytes 6382592 | tf_op jit(solution)/shard_map/while/body/reduce_sum | solution.py:106
  147.1 0.8 copy.76
  147.9 24.5 %scatter_custom_fusion = f32[65,8192]{0,1:T(8,128)} fusion(s32[4096]{0:T(1024)S(1)} %bitcast.99, f32[4096,65]{1,0:T(8,128)S(1)} %bitcast.95, f32[]{:T(128)} %constant.142.clone.1), kind=kCustom, calls=%fused_computation.75 | custom fusion | flops 266240 | bytes 2129924 | tf_op jit(solution)/shard_map/scatter-add | solution.py:160
  172.4 1.6 slice-done
  174.0 0.9 copy.72
  174.9 14.3 %collective-permute-start.1 = (f32[65,4096]{1,0:T(8,128)S(1)}, f32[65,4096]{1,0:T(8,128)}, u32[]{:S(2)}, u32[]{:S(2)}) collective-permute-start(f32[65,4096]{1,0:T(8,128)S(1)} %copy.72), channel_id=1, source_target_pairs={{1,0},{2,1},{3,2},{4,3},{5,4},{6,5},{7,6},{8,7},{9,8},{10,9},{11,1... | collective-permute-start | bytes 3194888 | tf_op jit(solution)/shard_map/ppermute | solution.py:12
  189.3 13.7 %collective-permute-done.1 = f32[65,4096]{1,0:T(8,128)} collective-permute-done((f32[65,4096]{1,0:T(8,128)S(1)}, f32[65,4096]{1,0:T(8,128)}, u32[]{:S(2)}, u32[]{:S(2)}) %collective-permute-start.1) | collective-permute-done | bytes 1064992 | tf_op jit(solution)/shard_map/ppermute | solution.py:12
  203.0 1.8 copy.73
  204.8 3.1 %slice_add_fusion = f32[65,4096]{0,1:T(8,128)} fusion(f32[65,4096]{0,1:T(8,128)S(1)} %copy.73, f32[65,8192]{0,1:T(8,128)} %scatter_custom_fusion), kind=kLoop, calls=%fused_computation.72 | loop fusion | flops 266240 | bytes 3194880 | tf_op jit(solution)/shard_map/add | solution.py:163
  207.9 82.4 %reduce-scatter.2.cloned.1.call-done = f32[65,256]{0,1:T(8,128)} async-done(((f32[65,4096]{0,1:T(8,128)}), f32[65,256]{0,1:T(8,128)}) %reduce-scatter.2.cloned.1.call-update) | async-done | bytes 66576 | tf_op jit(solution)/shard_map/reduce_scatter | solution.py:162
  290.3 1.6 copy.74
  291.9 1.7 slice_reduce_fusion
  (66 shorter events, 7.2 us)
Async XLA Ops:
  7.2 119.5 %copy-start = (bf16[64,512]{1,0:T(8,128)(2,1)S(1)}, bf16[64,512]{1,0:T(8,128)(2,1)}, u32[]{:S(2)}) copy-start(bf16[64,512]{1,0:T(8,128)(2,1)} %param.18) | copy-start | bytes 196612
  7.2 17.4 %copy-start.3 = (s32[1,1,16]{2,1,0:T(1,128)S(1)}, s32[1,1,16]{2,1,0:T(1,128)}, u32[]{:S(2)}) copy-start(s32[1,1,16]{2,1,0:T(1,128)} %param.20) | copy-start | bytes 196
  7.2 18.7 %copy-start.4 = (f32[16,3]{0,1:T(4,128)S(1)}, f32[16,3]{0,1:T(4,128)}, u32[]{:S(2)}) copy-start(f32[16,3]{0,1:T(4,128)} %param.17) | copy-start | bytes 580
  7.2 20.9 %copy-start.2 = (s32[1,1,16,256]{3,2,1,0:T(8,128)S(1)}, s32[1,1,16,256]{3,2,1,0:T(8,128)}, u32[]{:S(2)}) copy-start(s32[1,1,16,256]{3,2,1,0:T(8,128)} %param.19) | copy-start | bytes 49156
  7.2 94.5 %all-gather.2.cloned.1.call-start = ((), (), s32[]{:S(2)}) async-start(), calls=%async_computation.1 | async-start | bytes 4456448 | tf_op jit(solution)/shard_map/all_gather | solution.py:148
  10.8 13.0 %collective-permute-start = (f32[69,256]{0,1:T(8,128)S(1)}, f32[69,256]{0,1:T(8,128)S(1)}, u32[]{:S(2)}, u32[]{:S(2)}) collective-permute-start(f32[69,256]{0,1:T(8,128)S(1)} %pad_maximum_fusion.2), channel_id=1, source_target_pairs={{0,1},{1,2},{2,3},{3,4},{4,5},{5,6},{6,7},{7,8},{8,9},{9,10},{10,1... | collective-permute-start | bytes 211976 | tf_op jit(solution)/shard_map/ppermute | solution.py:12
  24.5 265.8 %reduce-scatter.2.cloned.1.call-start = ((), (), s32[]{:S(2)}) async-start(), calls=%async_computation.2 | async-start | bytes 2228224 | tf_op jit(solution)/shard_map/reduce_scatter | solution.py:162
  126.7 2.2 copy-start.1
  172.4 1.6 slice-start
  174.9 28.0 %collective-permute-start.1 = (f32[65,4096]{1,0:T(8,128)S(1)}, f32[65,4096]{1,0:T(8,128)}, u32[]{:S(2)}, u32[]{:S(2)}) collective-permute-start(f32[65,4096]{1,0:T(8,128)S(1)} %copy.72), channel_id=1, source_target_pairs={{1,0},{2,1},{3,2},{4,3},{5,4},{6,5},{7,6},{8,7},{9,8},{10,9},{11,1... | collective-permute-start | bytes 3194888 | tf_op jit(solution)/shard_map/ppermute | solution.py:12
Sparse Core Ops, SparseCore 0:
  24.7 76.9 all-gather.1
  208.0 82.2 reduce-scatter.1
where the time goes:
time: 301 us; the launch traced here: 300 us
  waiting for transfers between devices  180 us (60%)
  other arithmetic  44.5 us (15%)
  local copies, waits for them, and re-layouts  30.8 us (10%)
  between operations  17.1 us (6%)
  starting transfers between devices  16.3 us (5%)
  matrix products  11.4 us (4%)
    reduce_scatter x1, waiting for transfers between devices, on_device(): lax.psum_scatter(totals[:, :block_rows] + returned, 'cam', scatter_dimens...  82.4 us
    all_gather x1, waiting for transfers between devices, on_device(): lax.all_gather(jnp.stack([own_slab, upper_slab]), 'cam', axis=2, tiled=True)  72.8 us
    ppermute x2, waiting for transfers between devices, shifted(): return lax.ppermute(shard, axis, pairs)  24.6 us
    scatter-add x1, other arithmetic, on_device(): jnp.zeros((channels + 1, 2 * block_rows), jnp.float32).at[:, entries]  24.5 us
    ppermute x2, starting transfers between devices, shifted(): return lax.ppermute(shard, axis, pairs)  16.2 us
    gather x2, local copies, waits for them, and re-layouts, on_device(): gathered = jnp.take(gauss_table, entries, axis=1)  14 us
  transfers between devices with their start and end apart: 4, of which 4 were waited for; matrix products, arithmetic and copies ran while one was open for 1% of the time, Pallas kernels for 0%

commit v1 on v0

v1 whole, which is shorter than its diff:
```python
import jax
import jax.numpy as jnp
from jax import lax
from jax.experimental import pallas as pl
from jax.experimental.pallas import tpu as pltpu
from jax.sharding import PartitionSpec as P

TS = 16
F32 = jnp.float32
BF16 = jnp.bfloat16
DEAD = 512.0
NN = (((1,), (0,)), ((), ()))
NT = (((1,), (1,)), ((), ()))
LOG2E = 1.4426950408889634


def dot(left, right, dims):
    return lax.dot_general(left, right, dims, preferred_element_type=F32)


def rolled(shard, axis, by):
    length = lax.axis_size(axis)
    return lax.ppermute(shard, axis, [(i, (i + by) % length) for i in range(length)])


def pieces(value):
    first = value.astype(BF16).astype(F32)
    rest = value - first
    second = rest.astype(BF16).astype(F32)
    third = (rest - second).astype(BF16).astype(F32)
    return first, second, third


def pack_kernel(ids_ref, counts_ref, decoder_ref, targets_ref, out_ref, codes_ref):
    tile = pl.program_id(0)
    tiles, length = ids_ref.shape
    segment = length // 8

    @pl.when(tile == 0)
    def _():
        ids = ids_ref[...]
        row = lax.broadcasted_iota(jnp.int32, (tiles, length), 0)
        entry = lax.broadcasted_iota(jnp.int32, (tiles, length), 1)
        above = ids >= tiles * length
        inside = jnp.where(above, ids - tiles * length, ids) - row * length
        code = jnp.where(above, -1 - inside, inside).astype(F32)
        code = jnp.where(entry < counts_ref[...], code, DEAD)
        source = lax.broadcasted_iota(jnp.int32, (length, length), 0)
        place = lax.broadcasted_iota(jnp.int32, (length, length), 1)
        chosen = source == segment * (place % 8) + place // 8
        codes_ref[...] = dot(code.astype(BF16), chosen.astype(F32).astype(BF16), NN)

    out_ref[0, 0:64, :] = dot(decoder_ref[...], targets_ref[0], NT)
    out_ref[0, 64:72, :] = jnp.broadcast_to(codes_ref[pl.ds(tile, 1), :], (8, length))


def prep_kernel(camera_ref, place_ref, own_ref, upper_ref, feature_ref, terms_ref, row_ref):
    channels, length = feature_ref.shape[0], own_ref.shape[1]
    feature_ref[:, 0:length] = own_ref[0:channels, :].astype(BF16)
    feature_ref[:, length:] = upper_ref[0:channels, :].astype(BF16)

    def both(row):
        return jnp.concatenate(
            [own_ref[row : row + 1, :], upper_ref[row : row + 1, :]], axis=1
        )

    place_x, place_y, depth, spread, logit = (both(channels + i) for i in range(5))
    log_open = LOG2E * (
        jnp.log(0.99) - (jnp.maximum(-logit, 0.0) + jnp.log(1.0 + jnp.exp(-jnp.abs(logit))))
    )
    row_ref[...] = jnp.zeros(row_ref.shape, F32)
    centre_u, centre_v = place_ref[0], place_ref[1]
    for view in range(terms_ref.shape[0]):
        distance = depth - 0.05 * camera_ref[view, 2]
        u = (place_x - 0.75 * TS * camera_ref[view, 0]) / distance + centre_u
        v = (place_y - 0.75 * TS * camera_ref[view, 1]) / distance + centre_v
        radius = spread / distance
        inverse = (0.5 * LOG2E) / (radius * radius)
        terms = (log_open - inverse * (u * u + v * v), 2.0 * inverse * u, 2.0 * inverse * v, -inverse)
        for index, term in enumerate(terms):
            for turn, piece in enumerate(pieces(term)):
                at = 3 * index + turn
                row_ref[at : at + 1, :] = piece
        terms_ref[view] = row_ref[...].astype(BF16)


def shift_rows(value, by, fill, index):
    moved = pltpu.roll(value, by % 8, 0)
    inside = index >= by if by > 0 else index < 8 + by
    return jnp.where(inside, moved, fill)


def tile_work(
    packed, terms, features, squares_ref, basis_ref, own_ref, upper_ref, a_ref, w_ref, wb_ref, ct_ref, ts_ref
):
    channels = features.shape[0]
    length = packed.shape[1]
    steps = length // 8
    code = packed[channels : channels + 1, :]
    slot = lax.broadcasted_iota(jnp.int32, (2 * length, length), 0)
    wanted = jnp.where(slot < length, slot, length - 1 - slot).astype(F32)
    hot = jnp.where(wanted == code, 1.0, 0.0).astype(BF16)
    picked = dot(jnp.concatenate([features, terms], axis=0), hot, NN)
    feature_t = picked[0:channels].astype(BF16)
    line = lax.broadcasted_iota(jnp.int32, picked.shape, 0)
    dead = jnp.where(code == DEAD, -32768.0, 0.0)
    entry_rows = jnp.where(line == channels + 12, dead, picked).T.astype(BF16)
    a_ref[...] = jnp.exp2(dot(entry_rows, basis_ref[...], NN))

    index = lax.broadcasted_iota(jnp.int32, (8, length), 0)
    keep = jnp.ones((8, length), F32)
    for i in range(steps):
        rows = pl.ds(8 * i, 8)
        local = a_ref[rows, :] * keep
        w_ref[rows, :] = local
        keep = keep - local
    start = shift_rows(keep, 1, 1.0, index)
    for by in (1, 2, 4):
        start = start * shift_rows(start, by, 1.0, index)
    for i in range(steps // 2):
        rows = pl.ds(16 * i, 16)
        wb_ref[rows, :] = (w_ref[rows, :] * jnp.concatenate([start, start], axis=0)).astype(BF16)
    weight_bf = wb_ref[...]
    composite = dot(feature_t, weight_bf, NN).astype(BF16)
    pixel_grad = (
        dot(squares_ref[...], jnp.concatenate([composite] * 3, axis=0), NN) - packed[0:channels, :]
    ).astype(BF16)
    padded = jnp.concatenate([pixel_grad, jnp.zeros((16, length), BF16)], axis=0)
    ct_ref[...] = dot(entry_rows, padded, NN)

    total = jnp.zeros((8, length), F32)
    for i in range(steps):
        rows = pl.ds(8 * i, 8)
        total = total + w_ref[rows, :] * ct_ref[rows, :]
    scale = keep
    for by in (1, 2, 4):
        total = total + scale * shift_rows(total, -by, 0.0, index)
        scale = scale * shift_rows(scale, -by, 1.0, index)
    after = shift_rows(total, -1, 0.0, index)
    for i in reversed(range(steps)):
        rows = pl.ds(8 * i, 8)
        gap = ct_ref[rows, :] - after
        term = (w_ref[rows, :] * start) * gap
        after = after + a_ref[rows, :] * gap
        ts_ref[rows, :] = term[:, 0:128] + term[:, 128:256]
    sums = ts_ref[...]
    sums_hi = sums.astype(BF16)
    sums_lo = (sums - sums_hi.astype(F32)).astype(BF16)
    ones = jnp.ones((8, length), BF16)
    logit_row = dot(ones, jnp.concatenate([sums_hi, sums_lo], axis=1), NT)
    feature_grad = dot(pixel_grad, weight_bf, NT)
    grad_hi = feature_grad.astype(BF16)
    grad_lo = (feature_grad - grad_hi.astype(F32)).astype(BF16)
    logit_hi = logit_row.astype(BF16).astype(F32)
    logit_both = jnp.concatenate([logit_hi, logit_row - logit_hi], axis=0).astype(BF16)
    values = jnp.concatenate([grad_hi, grad_lo, logit_both], axis=0)
    spread = dot(values, hot, NT)
    c = channels
    for ref, first in ((own_ref, 0), (upper_ref, length)):
        part = spread[:, first : first + length]
        ref[0:c, :] += part[0:c] + part[c : 2 * c]
        ref[c : c + 8, :] += part[2 * c : 2 * c + 8] + part[2 * c + 8 : 2 * c + 16]


def main_kernel(
    packed_ref, terms_ref, feature_ref, decoder_ref, own_ref, upper_ref, squares_ref, basis_ref, *scratch
):
    channels, length = feature_ref.shape[0], packed_ref.shape[2]

    @pl.when(pl.program_id(0) == 0)
    def _():
        own_ref[...] = jnp.zeros(own_ref.shape, F32)
        upper_ref[...] = jnp.zeros(upper_ref.shape, F32)
        for turn, piece in enumerate(pieces(dot(decoder_ref[...], decoder_ref[...], NT))):
            squares_ref[:, channels * turn : channels * (turn + 1)] = piece.astype(BF16)
        line = lax.broadcasted_iota(jnp.int32, basis_ref.shape, 0) - channels
        pixel = lax.broadcasted_iota(jnp.int32, basis_ref.shape, 1)
        px = (pixel % TS).astype(F32) - (0.5 * TS - 0.5)
        py = (pixel // TS).astype(F32) - (0.5 * TS - 0.5)
        basis = jnp.where(line < 3, 1.0, jnp.where(line < 6, px, jnp.where(line < 9, py, px * px + py * py)))
        basis = jnp.where(line == 12, 1.0, basis)
        basis_ref[...] = jnp.where((line < 0) | (line > 12), 0.0, basis).astype(BF16)

    for turn in range(packed_ref.shape[0]):
        tile_work(
            packed_ref[turn],
            terms_ref[turn],
            feature_ref[...],
            squares_ref,
            basis_ref,
            own_ref,
            upper_ref,
            *(ref.at[turn] for ref in scratch),
        )


def on_device(features, positions, spreads, logits, camera, decoder, tile_lists, counts, targets):
    channels, length = features.shape
    tiles = tile_lists.shape[2]
    decoded = decoder.shape[1]
    views = camera.shape[0]
    group = 2
    column = lax.axis_index("cam")
    tile_row = lax.axis_index("space")
    image_width = TS * lax.axis_size("cam")
    image_height = TS * lax.axis_size("space")

    packed = pl.pallas_call(
        pack_kernel,
        out_shape=jax.ShapeDtypeStruct((tiles, channels + 8, length), F32),
        grid=(tiles,),
        in_specs=[
            pl.BlockSpec((tiles, length), lambda t: (0, 0)),
            pl.BlockSpec((tiles, 1), lambda t: (0, 0)),
            pl.BlockSpec((channels, decoded), lambda t: (0, 0)),
            pl.BlockSpec((1, length, decoded), lambda t: (t, 0, 0)),
        ],
        out_specs=pl.BlockSpec((1, channels + 8, length), lambda t: (t, 0, 0)),
        scratch_shapes=[pltpu.VMEM((tiles, length), F32)],
        cost_estimate=pl.CostEstimate(
            flops=2 * tiles * length * channels * decoded,
            bytes_accessed=tiles * length * (2 * decoded + 4 * channels),
            transcendentals=0,
        ),
        name="pack",
    )(tile_lists[0, 0], counts[0, 0][:, None], decoder, targets[0, 0])
    received = lax.all_to_all(packed, "cam", 0, 0, tiled=True)

    own_slab = jnp.concatenate([features, positions, spreads[None], logits[None]], axis=0)
    upper_slab = rolled(own_slab, "space", 1)
    place = jnp.stack(
        [
            0.5 * image_width - (column * TS + 0.5 * TS),
            0.5 * image_height - (tile_row * TS + 0.5 * TS),
        ]
    ).astype(F32)
    feature_bf, terms = pl.pallas_call(
        prep_kernel,
        out_shape=(
            jax.ShapeDtypeStruct((channels, 2 * length), BF16),
            jax.ShapeDtypeStruct((views, 16, 2 * length), BF16),
        ),
        in_specs=[
            pl.BlockSpec(memory_space=pltpu.SMEM),
            pl.BlockSpec(memory_space=pltpu.SMEM),
            pl.BlockSpec(memory_space=pltpu.VMEM),
            pl.BlockSpec(memory_space=pltpu.VMEM),
        ],
        out_specs=(
            pl.BlockSpec(memory_space=pltpu.VMEM),
            pl.BlockSpec(memory_space=pltpu.VMEM),
        ),
        scratch_shapes=[pltpu.VMEM((16, 2 * length), F32)],
        cost_estimate=pl.CostEstimate(flops=10000000, bytes_accessed=1000000, transcendentals=20000),
        name="prep",
    )(camera, place, own_slab, upper_slab)

    own_sum, upper_sum = pl.pallas_call(
        main_kernel,
        out_shape=(jax.ShapeDtypeStruct((channels + 8, length), F32),) * 2,
        grid=(views // group,),
        in_specs=[
            pl.BlockSpec((group, channels + 8, length), lambda t: (t, 0, 0)),
            pl.BlockSpec((group, 16, 2 * length), lambda t: (t, 0, 0)),
            pl.BlockSpec((channels, 2 * length), lambda t: (0, 0)),
            pl.BlockSpec((channels, decoded), lambda t: (0, 0)),
        ],
        out_specs=(pl.BlockSpec((channels + 8, length), lambda t: (0, 0)),) * 2,
        scratch_shapes=[
            pltpu.VMEM((channels, 3 * channels), BF16),
            pltpu.VMEM((channels + 16, length), BF16),
            pltpu.VMEM((group, length, length), F32),
            pltpu.VMEM((group, length, length), F32),
            pltpu.VMEM((group, length, length), BF16),
            pltpu.VMEM((group, length, length), F32),
            pltpu.VMEM((group, length, 128), F32),
        ],
        cost_estimate=pl.CostEstimate(
            flops=views * 2 * length * length * 1000, bytes_accessed=2000000, transcendentals=views * length * length
        ),
        name="splat",
    )(received, terms, feature_bf, decoder)
    returned = rolled(upper_sum, "space", -1)
    summed = own_sum + returned
    return summed[:channels], summed[channels] * (1.0 - jax.nn.sigmoid(logits))


def solution(mesh):
    placed = (
        P(None, ("cam", "space")),
        P(None, ("cam", "space")),
        P(("cam", "space")),
        P(("cam", "space")),
        P(),
        P(),
        P("cam", "space", None, None),
        P("cam", "space", None),
        P("cam", "space", None, None, None),
    )
    return jax.shard_map(
        on_device,
        mesh=mesh,
        in_specs=placed,
        out_specs=(P(None, ("cam", "space")), P(("cam", "space"))),
        check_vma=False,
    )
```

time: 301 us -> 90.1 us (0.30)
  the two profiles are of different devices: /device:TPU:4 before, /device:TPU:24 now
where the time goes in v1:
time: 90.1 us; the launch traced here: 89.5 us
  Pallas kernels  36.3 us (40%)
  waiting for transfers between devices  23.4 us (26%)
  starting transfers between devices  22.6 us (25%)
  local copies, waits for them, and re-layouts  4.33 us (5%)
  other arithmetic  2.15 us (2%)
    pallas_call x1, Pallas kernels, on_device(): pl.pallas_call(main_kernel, out_shape=(jax.ShapeDtypeStruct((channels + 8...  22.9 us
    ppermute x2, starting transfers between devices, rolled(): lax.ppermute(shard, axis, [(i, (i + by) % length) for i in range(length)])  13.4 us
    ppermute x2, waiting for transfers between devices, rolled(): lax.ppermute(shard, axis, [(i, (i + by) % length) for i in range(length)])  12.2 us
    all_to_all x1, waiting for transfers between devices, on_device(): received = lax.all_to_all(packed, 'cam', 0, 0, tiled=True)  11.2 us
    pallas_call x1, Pallas kernels, on_device(): pl.pallas_call(pack_kernel, out_shape=jax.ShapeDtypeStruct((tiles, channe...  11.1 us
    all_to_all x1, starting transfers between devices, on_device(): received = lax.all_to_all(packed, 'cam', 0, 0, tiled=True)  9.21 us
    unnamed x17, local copies, waits for them, and re-layouts  2.36 us
    pallas_call x1, Pallas kernels, on_device(): pl.pallas_call(prep_kernel, out_shape=(jax.ShapeDtypeStruct((channels, 2...  2.33 us
  transfers between devices with their start and end apart: 3, of which 3 were waited for; matrix products, arithmetic and copies ran while one was open for 2% of the time, Pallas kernels for 3%

profile of v1, /device:TPU:24, one launch (start us, length us, event | category | flops | bytes accessed | tf_op | source)
XLA Modules:
  0.0 89.5 jit_solution(11671197215491557074)
XLA Ops:
  0.6 1.3 %copy.11.counts_ref = s32[16,1]{1,0:T(8,128)} copy(s32[16,1]{0,1:T(1,128)} %bitcast.13) | data formatting | bytes 128 | tf_op jit(solution)/shard_map/broadcast_in_dim;squeeze | solution.py:226
  2.0 11.1 %pack.1 = f32[16,72,256]{2,1,0:T(8,128)} custom-call(s32[16,256]{1,0:T(8,128)} %bitcast.9, s32[16,1]{1,0:T(8,128)} %copy.11.counts_ref, bf16[64,512]{1,0:T(8,128)(2,1)} %decoder_ref.3, bf16[16,256,512]{2,1,0:T(8,128)(2,1)} %bitcast.8), custom_call_target="tpu_custom_call" | custom-call | flops 268435456 | bytes 5242880 | tf_op jit(solution)/shard_map/pack/pallas_call | solution.py:208
  13.0 0.0 copy-start.3
  13.0 0.0 copy-start.4
  13.0 0.0 copy-start.5
  13.0 0.0 copy-start.7
  13.0 0.0 copy-start.6
  13.0 9.2 %all-to-all-start = ((f32[16,72,256]{2,1,0:T(8,128)}), f32[16,72,256]{2,1,0:T(8,128)S(1)}, u32[]{:S(2)}, u32[]{:S(2)}) async-start(f32[16,72,256]{2,1,0:T(8,128)} %pack.1), calls=%async_computation | async-start | bytes 2359296 | tf_op jit(solution)/shard_map/all_to_all | solution.py:227
  22.3 0.0 copy-done.3
  22.3 0.0 copy-done.4
  22.3 0.0 copy-done.5
  22.3 0.0 copy-done.7
  22.3 0.0 copy-start.1
  22.3 1.9 %collective-permute-start = (f32[69,256]{1,0:T(8,128)S(1)}, f32[69,256]{1,0:T(8,128)S(1)}, u32[]{:S(2)}, u32[]{:S(2)}) collective-permute-start(f32[69,256]{1,0:T(8,128)S(1)} %pad_maximum_fusion.own_ref), channel_id=1, source_target_pairs={{0,1},{1,2},{2,3},{3,4},{4,5},{5,6},{6,7},{7,8},{8,9},{9,10},{10,1... | collective-permute-start | bytes 211976 | tf_op jit(solution)/shard_map/ppermute | solution.py:23
  24.3 0.0 copy-done.6
  24.3 0.7 copy.12.camera_ref
  24.9 0.7 pad_maximum_fusion.1.place_ref
  25.6 9.9 %collective-permute-done.upper_ref = f32[69,256]{1,0:T(8,128)S(1)} collective-permute-done((f32[69,256]{1,0:T(8,128)S(1)}, f32[69,256]{1,0:T(8,128)S(1)}, u32[]{:S(2)}, u32[]{:S(2)}) %collective-permute-start) | collective-permute-done | bytes 70688 | tf_op jit(solution)/shard_map/ppermute | solution.py:23
  35.5 0.0 copy-done.1
  35.5 0.0 copy-start.2
  35.5 0.6 copy-done.2
  36.2 2.3 %prep.1 = (bf16[64,512]{1,0:T(8,128)(2,1)}, bf16[16,16,512]{2,1,0:T(8,128)(2,1)}) custom-call(f32[16,3]{1,0:T(8,128)} %copy.12.camera_ref, f32[2]{0:T(128)} %pad_maximum_fusion.1.place_ref, f32[69,256]{1,0:T(8,128)} %copy-done.1, f32[69,256]{1,0:T(8,128)} %copy-done.2), custom_call_target="tpu_custom_call" | custom-call | flops 10000000 | bytes 1000000 | tf_op jit(solution)/shard_map/prep/pallas_call | solution.py:237
  38.5 11.2 %all-to-all-done.packed_ref = f32[16,72,256]{2,1,0:T(8,128)S(1)} async-done(((f32[16,72,256]{2,1,0:T(8,128)}), f32[16,72,256]{2,1,0:T(8,128)S(1)}, u32[]{:S(2)}, u32[]{:S(2)}) %all-to-all-start) | async-done | bytes 1179680 | tf_op jit(solution)/shard_map/all_to_all | solution.py:227
  49.7 0.0 copy-start
  49.7 1.0 %copy-done = f32[16,72,256]{2,1,0:T(8,128)} copy-done((f32[16,72,256]{2,1,0:T(8,128)}, f32[16,72,256]{2,1,0:T(8,128)S(1)}, u32[]{:S(2)}) %copy-start) | copy-done | bytes 1179672
  50.8 22.9 %splat.1 = (f32[72,256]{1,0:T(8,128)}, f32[72,256]{1,0:T(8,128)}) custom-call(f32[16,72,256]{2,1,0:T(8,128)} %copy-done, bf16[16,16,512]{2,1,0:T(8,128)(2,1)} %get-tuple-element.6.terms_ref, bf16[64,512]{1,0:T(8,128)(2,1)} %get-tuple-element.7.feature_ref, bf16[64,512]{1,0:T(8,128)(2,1)} %decoder_ref.3), custom_call_target="tpu_custom_call" | custom-call | flops 2097152000 | bytes 2000000 | tf_op jit(solution)/shard_map/splat/pallas_call | solution.py:258
  73.7 11.4 %collective-permute-start.1 = (f32[72,256]{1,0:T(8,128)}, f32[72,256]{1,0:T(8,128)S(1)}, u32[]{:S(2)}, u32[]{:S(2)}) collective-permute-start(f32[72,256]{1,0:T(8,128)} %get-tuple-element.9), channel_id=1, source_target_pairs={{0,31},{1,0},{2,1},{3,2},{4,3},{5,4},{6,5},{7,6},{8,7},{9,8},{10,9... | collective-permute-start | bytes 221192 | tf_op jit(solution)/shard_map/ppermute | solution.py:23
  85.1 2.3 %collective-permute-done.1 = f32[72,256]{1,0:T(8,128)S(1)} collective-permute-done((f32[72,256]{1,0:T(8,128)}, f32[72,256]{1,0:T(8,128)S(1)}, u32[]{:S(2)}, u32[]{:S(2)}) %collective-permute-start.1) | collective-permute-done | bytes 73760 | tf_op jit(solution)/shard_map/ppermute | solution.py:23
  87.4 0.9 %add.14 = f32[72,256]{1,0:T(8,128)S(1)} add(f32[72,256]{1,0:T(8,128)} %get-tuple-element.8, f32[72,256]{1,0:T(8,128)S(1)} %collective-permute-done.1) | non-fusion elementwise | flops 18432 | bytes 221184 | tf_op jit(solution)/shard_map/add | solution.py:284
  88.3 0.6 slice.8
  88.9 0.6 subtract_multiply_fusion
  (2 shorter events, 0.0 us)
Async XLA Ops:
  13.0 9.2 %copy-start.3 = (f32[64,256]{1,0:T(8,128)S(1)}, f32[64,256]{1,0:T(8,128)}, u32[]{:S(2)}) copy-start(f32[64,256]{1,0:T(8,128)} %param.9) | copy-start | bytes 196612
  13.0 9.2 %copy-start.4 = (f32[256]{0:T(256)S(1)}, f32[256]{0:T(256)}, u32[]{:S(2)}) copy-start(f32[256]{0:T(256)} %param.12) | copy-start | bytes 3076
  13.0 9.3 %copy-start.5 = (f32[3,256]{1,0:T(4,128)S(1)}, f32[3,256]{1,0:T(4,128)}, u32[]{:S(2)}) copy-start(f32[3,256]{1,0:T(4,128)} %param.10) | copy-start | bytes 9220
  13.0 9.3 %copy-start.7 = (f32[256]{0:T(256)S(1)}, f32[256]{0:T(256)}, u32[]{:S(2)}) copy-start(f32[256]{0:T(256)} %param.11) | copy-start | bytes 3076
  13.0 11.2 %copy-start.6 = (f32[16,3]{0,1:T(4,128)S(1)}, f32[16,3]{0,1:T(4,128)}, u32[]{:S(2)}) copy-start(f32[16,3]{0,1:T(4,128)} %param.13) | copy-start | bytes 580
  13.0 36.7 %all-to-all-start = ((f32[16,72,256]{2,1,0:T(8,128)}), f32[16,72,256]{2,1,0:T(8,128)S(1)}, u32[]{:S(2)}, u32[]{:S(2)}) async-start(f32[16,72,256]{2,1,0:T(8,128)} %pack.1), calls=%async_computation | async-start | bytes 2359296 | tf_op jit(solution)/shard_map/all_to_all | solution.py:227
  22.3 13.2 %copy-start.1 = (f32[69,256]{1,0:T(8,128)}, f32[69,256]{1,0:T(8,128)S(1)}, u32[]{:S(2)}) copy-start(f32[69,256]{1,0:T(8,128)S(1)} %pad_maximum_fusion.own_ref) | copy-start | bytes 211972
  22.3 13.2 %collective-permute-start = (f32[69,256]{1,0:T(8,128)S(1)}, f32[69,256]{1,0:T(8,128)S(1)}, u32[]{:S(2)}, u32[]{:S(2)}) collective-permute-start(f32[69,256]{1,0:T(8,128)S(1)} %pad_maximum_fusion.own_ref), channel_id=1, source_target_pairs={{0,1},{1,2},{2,3},{3,4},{4,5},{5,6},{6,7},{7,8},{8,9},{9,10},{10,1... | collective-permute-start | bytes 211976 | tf_op jit(solution)/shard_map/ppermute | solution.py:23
  35.5 0.6 copy-start.2
  49.7 1.0 %copy-start = (f32[16,72,256]{2,1,0:T(8,128)}, f32[16,72,256]{2,1,0:T(8,128)S(1)}, u32[]{:S(2)}) copy-start(f32[16,72,256]{2,1,0:T(8,128)S(1)} %all-to-all-done.packed_ref) | copy-start | bytes 3538948
  73.7 13.7 %collective-permute-start.1 = (f32[72,256]{1,0:T(8,128)}, f32[72,256]{1,0:T(8,128)S(1)}, u32[]{:S(2)}, u32[]{:S(2)}) collective-permute-start(f32[72,256]{1,0:T(8,128)} %get-tuple-element.9), channel_id=1, source_target_pairs={{0,31},{1,0},{2,1},{3,2},{4,3},{5,4},{6,5},{7,6},{8,7},{9,8},{10,9... | collective-permute-start | bytes 221192 | tf_op jit(solution)/shard_map/ppermute | solution.py:23

commit v2 on v1

v2 whole, which is shorter than its diff:
```python
import jax
import jax.numpy as jnp
from jax import lax
from jax.experimental import pallas as pl
from jax.experimental.pallas import tpu as pltpu
from jax.sharding import PartitionSpec as P

TS = 16
F32 = jnp.float32
BF16 = jnp.bfloat16
DEAD = 512.0
FULL = 32000.0
NN = (((1,), (0,)), ((), ()))
NT = (((1,), (1,)), ((), ()))
LOG2E = 1.4426950408889634


def dot(left, right, dims):
    return lax.dot_general(left, right, dims, preferred_element_type=F32)


def shifted(shard, axis, by):
    length = lax.axis_size(axis)
    pairs = [(i, i + by) for i in range(length) if 0 <= i + by < length]
    return lax.ppermute(shard, axis, pairs)


def pieces(value):
    first = value.astype(BF16).astype(F32)
    rest = value - first
    second = rest.astype(BF16).astype(F32)
    third = (rest - second).astype(BF16).astype(F32)
    return first, second, third


def list_kernel(ids_ref, counts_ref, out_ref):
    tiles, length = ids_ref.shape
    segment = length // 8
    ids = ids_ref[...]
    row = lax.broadcasted_iota(jnp.int32, (tiles, length), 0)
    entry = lax.broadcasted_iota(jnp.int32, (tiles, length), 1)
    above = ids >= tiles * length
    inside = jnp.where(above, ids - tiles * length, ids) - row * length
    code = jnp.where(above, -1 - inside, inside).astype(F32)
    live = jnp.zeros((tiles, length), jnp.int32)
    for tile in range(tiles):
        live = jnp.where(row == tile, counts_ref[tile], live)
    code = jnp.where(entry < live, code, DEAD)
    source = lax.broadcasted_iota(jnp.int32, (length, length), 0)
    place = lax.broadcasted_iota(jnp.int32, (length, length), 1)
    chosen = source == segment * (place % 8) + place // 8
    codes = dot(code.astype(BF16), chosen.astype(F32).astype(BF16), NN).astype(jnp.int32)
    for tile in range(tiles):
        out_ref[tile] = jnp.broadcast_to(codes[tile : tile + 1, :], (8, length)).astype(jnp.int16)


def pack_kernel(decoder_ref, targets_ref, out_ref):
    channels = decoder_ref.shape[0]
    for turn in range(targets_ref.shape[0]):
        value = dot(targets_ref[turn], decoder_ref[...], NT).T
        largest = jnp.max(jnp.abs(value), axis=0, keepdims=True)
        power = jnp.floor(jnp.log2(jnp.maximum(largest, 1e-30))) + 1.0
        fixed = jnp.round(value * (FULL * jnp.exp2(-power)))
        out_ref[turn, 0:channels, :] = fixed.astype(jnp.int32).astype(jnp.int16)
        powers = jnp.broadcast_to(power, (8, value.shape[1]))
        out_ref[turn, channels : channels + 8, :] = powers.astype(jnp.int32).astype(jnp.int16)


def prep_kernel(camera_ref, place_ref, own_ref, upper_ref, feature_ref, terms_ref, row_ref):
    channels, length = feature_ref.shape[0], own_ref.shape[1]
    feature_ref[:, 0:length] = own_ref[0:channels, :].astype(BF16)
    feature_ref[:, length:] = upper_ref[0:channels, :].astype(BF16)

    def both(row):
        own = own_ref[row : row + 1, :]
        return jnp.concatenate([own, jnp.where(place_ref[2] > 0.0, upper_ref[row : row + 1, :], own)], axis=1)

    place_x, place_y, depth, spread, logit = (both(channels + i) for i in range(5))
    log_open = LOG2E * (
        jnp.log(0.99) - (jnp.maximum(-logit, 0.0) + jnp.log(1.0 + jnp.exp(-jnp.abs(logit))))
    )
    row_ref[...] = jnp.zeros(row_ref.shape, F32)
    centre_u, centre_v = place_ref[0], place_ref[1]
    for view in range(terms_ref.shape[0]):
        distance = depth - 0.05 * camera_ref[view, 2]
        u = (place_x - 0.75 * TS * camera_ref[view, 0]) / distance + centre_u
        v = (place_y - 0.75 * TS * camera_ref[view, 1]) / distance + centre_v
        radius = spread / distance
        inverse = (0.5 * LOG2E) / (radius * radius)
        terms = (log_open - inverse * (u * u + v * v), 2.0 * inverse * u, 2.0 * inverse * v, -inverse)
        for index, term in enumerate(terms):
            for turn, piece in enumerate(pieces(term)):
                at = 3 * index + turn
                row_ref[at : at + 1, :] = piece
        terms_ref[view] = row_ref[...].astype(BF16)


def shift_rows(value, by, fill, index):
    moved = pltpu.roll(value, by % 8, 0)
    inside = index >= by if by > 0 else index < 8 + by
    return jnp.where(inside, moved, fill)


def in_turns(works):
    works = list(works)
    while works:
        works = [work for work in works if next(work, None) is not None]


def hot_rows(wanted_ref, codes, hot_ref):
    code = jnp.concatenate([codes, codes], axis=0).astype(BF16)
    half = wanted_ref.shape[1]
    one, zero = jnp.ones((16, half), BF16), jnp.zeros((16, half), BF16)
    for first in range(0, hot_ref.shape[0], 16):
        wanted = wanted_ref[first : first + 16, :]
        for side in range(0, code.shape[1], half):
            hot_ref[first : first + 16, side : side + half] = jnp.where(
                wanted == code[:, side : side + half], one, zero
            )


def set_wanted(wanted_ref):
    slot = lax.broadcasted_iota(jnp.int32, wanted_ref.shape, 0)
    length = wanted_ref.shape[0] // 2
    wanted_ref[...] = jnp.where(slot < length, slot, length - 1 - slot).astype(F32).astype(BF16)


def forward_tile(
    codes_ref, terms_ref, feature_ref, squares_ref, basis_ref, wanted_ref,
    entry_ref, a_ref, w_ref, wb_ref, ends_ref, projected_ref, hot_ref
):
    channels = feature_ref.shape[0]
    length = codes_ref.shape[1]
    steps = length // 8
    codes = codes_ref[...].astype(jnp.int32).astype(F32)
    hot_rows(wanted_ref, codes, hot_ref)
    yield True
    table = jnp.concatenate([feature_ref[...], terms_ref[...]], axis=0)
    picked = dot(table, hot_ref[...], NN)
    feature_t = picked[0:channels].astype(BF16)
    line = lax.broadcasted_iota(jnp.int32, (16, length), 0)
    dead = jnp.where(codes[0:1, :] == DEAD, -32768.0, 0.0)
    lower = jnp.where(line == 12, dead, picked[channels:])
    entry_ref[...] = jnp.concatenate([picked[0:channels], lower], axis=0).T.astype(BF16)
    yield True
    for first in range(0, length, 64):
        a_ref[first : first + 64, :] = jnp.exp2(dot(entry_ref[first : first + 64, :], basis_ref[...], NN))
    yield True
    index = lax.broadcasted_iota(jnp.int32, (8, length), 0)
    keep = jnp.ones((8, length), F32)
    for i in range(steps):
        rows = pl.ds(8 * i, 8)
        local = a_ref[rows, :] * keep
        w_ref[rows, :] = local
        keep = keep - local
    start = shift_rows(keep, 1, 1.0, index)
    for by in (1, 2, 4):
        start = start * shift_rows(start, by, 1.0, index)
    ends_ref[0:8, :] = start
    ends_ref[8:16, :] = keep
    yield True
    for i in range(steps // 2):
        rows = pl.ds(16 * i, 16)
        wb_ref[rows, :] = (w_ref[rows, :] * jnp.concatenate([start, start], axis=0)).astype(BF16)
    yield True
    composite = dot(feature_t, wb_ref[...], NN).astype(BF16)
    projected_ref[...] = dot(squares_ref[...], jnp.concatenate([composite] * 3, axis=0), NN)


def forward_kernel(
    codes_ref, terms_ref, feature_ref, decoder_ref,
    entry_ref, a_ref, w_ref, wb_ref, ends_ref, projected_ref,
    squares_ref, basis_ref, wanted_ref, hot_ref
):
    channels = feature_ref.shape[0]

    @pl.when(pl.program_id(0) == 0)
    def _():
        set_wanted(wanted_ref)
        for turn, piece in enumerate(pieces(dot(decoder_ref[...], decoder_ref[...], NT))):
            squares_ref[:, channels * turn : channels * (turn + 1)] = piece.astype(BF16)
        line = lax.broadcasted_iota(jnp.int32, basis_ref.shape, 0) - channels
        pixel = lax.broadcasted_iota(jnp.int32, basis_ref.shape, 1)
        px = (pixel % TS).astype(F32) - (0.5 * TS - 0.5)
        py = (pixel // TS).astype(F32) - (0.5 * TS - 0.5)
        basis = jnp.where(line < 3, 1.0, jnp.where(line < 6, px, jnp.where(line < 9, py, px * px + py * py)))
        basis = jnp.where(line == 12, 1.0, basis)
        basis_ref[...] = jnp.where((line < 0) | (line > 12), 0.0, basis).astype(BF16)

    in_turns(
        forward_tile(
            codes_ref.at[turn], terms_ref.at[turn],
            feature_ref, squares_ref, basis_ref, wanted_ref,
            *(ref.at[turn] for ref in (entry_ref, a_ref, w_ref, wb_ref, ends_ref, projected_ref, hot_ref)),
        )
        for turn in range(hot_ref.shape[0])
    )


def backward_tile(
    packed_ref, codes_ref, entry_ref, a_ref, w_ref, wb_ref, ends_ref, projected_ref, wanted_ref,
    own_ref, upper_ref, hot_ref, ct_ref, ts_ref
):
    channels, length = projected_ref.shape
    steps = length // 8
    index = lax.broadcasted_iota(jnp.int32, (8, length), 0)
    packed = packed_ref[...].astype(jnp.int32).astype(F32)
    scale = jnp.exp2(packed[channels : channels + 1, :]) * (1.0 / FULL)
    pixel_grad = (projected_ref[...] - packed[0:channels] * scale).astype(BF16)
    padded = jnp.concatenate([pixel_grad, jnp.zeros((16, length), BF16)], axis=0)
    yield True
    total = jnp.zeros((8, length), F32)
    for first in range(0, length, 64):
        ct = dot(entry_ref[first : first + 64, :], padded, NN)
        ct_ref[first : first + 64, :] = ct
        for i in range(8):
            total = total + w_ref[pl.ds(first + 8 * i, 8), :] * ct[8 * i : 8 * i + 8, :]
    yield True
    start, factor = ends_ref[0:8, :], ends_ref[8:16, :]
    for by in (1, 2, 4):
        total = total + factor * shift_rows(total, -by, 0.0, index)
        factor = factor * shift_rows(factor, -by, 1.0, index)
    after = shift_rows(total, -1, 0.0, index)
    for i in reversed(range(steps)):
        rows = pl.ds(8 * i, 8)
        gap = ct_ref[rows, :] - after
        term = (w_ref[rows, :] * start) * gap
        after = after + a_ref[rows, :] * gap
        ts_ref[rows, :] = term[:, 0:128] + term[:, 128:256]
    yield True
    feature_grad = dot(pixel_grad, wb_ref[...], NT)
    hot_rows(wanted_ref, codes_ref[...].astype(jnp.int32).astype(F32), hot_ref)
    yield True
    sums = ts_ref[...]
    sums_hi = sums.astype(BF16)
    sums_lo = (sums - sums_hi.astype(F32)).astype(BF16)
    ones = jnp.ones((8, length), BF16)
    logit_row = dot(ones, jnp.concatenate([sums_hi, sums_lo], axis=1), NT)
    grad_hi = feature_grad.astype(BF16)
    grad_lo = (feature_grad - grad_hi.astype(F32)).astype(BF16)
    logit_hi = logit_row.astype(BF16).astype(F32)
    logit_both = jnp.concatenate([logit_hi, logit_row - logit_hi], axis=0).astype(BF16)
    values = jnp.concatenate([grad_hi, grad_lo, logit_both], axis=0)
    yield True
    spread = dot(values, hot_ref[...], NT)
    c = channels
    for ref, first in ((own_ref, 0), (upper_ref, length)):
        part = spread[:, first : first + length]
        ref[0:c, :] += part[0:c] + part[c : 2 * c]
        ref[c : c + 8, :] += part[2 * c : 2 * c + 8] + part[2 * c + 8 : 2 * c + 16]


def backward_kernel(
    packed_ref, codes_ref, entry_ref, a_ref, w_ref, wb_ref, ends_ref, projected_ref,
    own_ref, upper_ref, wanted_ref, hot_ref, ct_ref, ts_ref
):
    @pl.when(pl.program_id(0) == 0)
    def _():
        set_wanted(wanted_ref)
        own_ref[...] = jnp.zeros(own_ref.shape, F32)
        upper_ref[...] = jnp.zeros(upper_ref.shape, F32)

    in_turns(
        backward_tile(
            *(
                ref.at[turn]
                for ref in (packed_ref, codes_ref, entry_ref, a_ref, w_ref, wb_ref, ends_ref, projected_ref)
            ),
            wanted_ref, own_ref, upper_ref, hot_ref.at[turn], ct_ref.at[turn], ts_ref.at[turn],
        )
        for turn in range(hot_ref.shape[0])
    )


def finish_kernel(own_ref, returned_ref, logits_ref, feature_ref, logit_ref):
    channels = feature_ref.shape[0]
    feature_ref[...] = own_ref[0:channels, :] + returned_ref[0:channels, :]
    summed = own_ref[channels : channels + 1, :] + returned_ref[channels : channels + 1, :]
    logit_ref[...] = summed / (1.0 + jnp.exp(logits_ref[...]))


def whole():
    return pl.BlockSpec(memory_space=pltpu.VMEM)


def small():
    return pltpu.CompilerParams(vmem_limit_bytes=8 << 20)


def blocks(group, *shape):
    return pl.BlockSpec((group,) + shape, lambda t: (t,) + (0,) * len(shape))


def fixed(*shape):
    return pl.BlockSpec(shape, lambda t: (0,) * len(shape))


def on_device(features, positions, spreads, logits, camera, decoder, tile_lists, counts, targets):
    channels, length = features.shape
    tiles = tile_lists.shape[2]
    decoded = decoder.shape[1]
    views = camera.shape[0]
    pack_group, group = 2, 2
    column = lax.axis_index("cam")
    tile_row = lax.axis_index("space")
    image_width = TS * lax.axis_size("cam")
    image_height = TS * lax.axis_size("space")
    shape = jax.ShapeDtypeStruct

    coded = pl.pallas_call(
        list_kernel,
        out_shape=shape((tiles, 8, length), jnp.int16),
        in_specs=[whole(), pl.BlockSpec(memory_space=pltpu.SMEM)],
        out_specs=whole(),
        compiler_params=small(),
        cost_estimate=pl.CostEstimate(flops=1000000, bytes_accessed=100000, transcendentals=0),
        name="lists",
    )(tile_lists[0, 0], counts[0, 0])
    codes = lax.all_to_all(coded, "cam", 0, 0, tiled=True)
    own_slab = jnp.concatenate([features, positions, spreads[None], logits[None]], axis=0)
    upper_slab = shifted(own_slab, "space", 1)

    packed = pl.pallas_call(
        pack_kernel,
        out_shape=shape((tiles, channels + 8, length), jnp.int16),
        grid=(tiles // pack_group,),
        in_specs=[fixed(channels, decoded), blocks(pack_group, length, decoded)],
        out_specs=blocks(pack_group, channels + 8, length),
        cost_estimate=pl.CostEstimate(
            flops=2 * tiles * length * channels * decoded,
            bytes_accessed=tiles * length * (2 * decoded + 2 * channels),
            transcendentals=0,
        ),
        name="pack",
    )(decoder, targets[0, 0])
    packed, upper_slab = lax.optimization_barrier((packed, upper_slab))
    received = lax.all_to_all(packed, "cam", 0, 0, tiled=True)

    place = jnp.stack(
        [
            0.5 * image_width - (column * TS + 0.5 * TS),
            0.5 * image_height - (tile_row * TS + 0.5 * TS),
            tile_row,
        ]
    ).astype(F32)
    feature_bf, terms = pl.pallas_call(
        prep_kernel,
        out_shape=(shape((channels, 2 * length), BF16), shape((views, 16, 2 * length), BF16)),
        in_specs=[
            pl.BlockSpec(memory_space=pltpu.SMEM),
            pl.BlockSpec(memory_space=pltpu.SMEM),
            whole(),
            whole(),
        ],
        out_specs=(whole(), whole()),
        scratch_shapes=[pltpu.VMEM((16, 2 * length), F32)],
        cost_estimate=pl.CostEstimate(flops=10000000, bytes_accessed=1000000, transcendentals=20000),
        name="prep",
    )(camera, place, own_slab, upper_slab)

    kept = (
        ((length, channels + 16), BF16),
        ((length, length), F32),
        ((length, length), F32),
        ((length, length), BF16),
        ((16, length), F32),
        ((channels, length), F32),
    )
    saved = pl.pallas_call(
        forward_kernel,
        out_shape=tuple(shape((views,) + size, kind) for size, kind in kept),
        grid=(views // group,),
        in_specs=[
            blocks(group, 8, length),
            blocks(group, 16, 2 * length),
            fixed(channels, 2 * length),
            fixed(channels, decoded),
        ],
        out_specs=tuple(blocks(group, *size) for size, _ in kept),
        scratch_shapes=[
            pltpu.VMEM((channels, 3 * channels), BF16),
            pltpu.VMEM((channels + 16, length), BF16),
            pltpu.VMEM((2 * length, 128), BF16),
            pltpu.VMEM((group, 2 * length, length), BF16),
        ],
        cost_estimate=pl.CostEstimate(
            flops=views * 2 * length * length * 600,
            bytes_accessed=views * length * length * 11,
            transcendentals=views * length * length,
        ),
        name="forward",
    )(codes, terms, feature_bf, decoder)

    own_sum, upper_sum = pl.pallas_call(
        backward_kernel,
        out_shape=(shape((channels + 8, length), F32),) * 2,
        grid=(views // group,),
        in_specs=[
            blocks(group, channels + 8, length),
            blocks(group, 8, length),
            *(blocks(group, *size) for size, _ in kept),
        ],
        out_specs=(whole(),) * 2,
        scratch_shapes=[
            pltpu.VMEM((2 * length, 128), BF16),
            pltpu.VMEM((group, 2 * length, length), BF16),
            pltpu.VMEM((group, length, length), F32),
            pltpu.VMEM((group, length, 128), F32),
        ],
        cost_estimate=pl.CostEstimate(
            flops=views * 2 * length * length * 600,
            bytes_accessed=views * length * length * 11,
            transcendentals=0,
        ),
        name="backward",
    )(received, codes, *saved)
    returned = shifted(upper_sum, "space", -1)
    grad_features, grad_logits = pl.pallas_call(
        finish_kernel,
        out_shape=(shape((channels, length), F32), shape((1, length), F32)),
        in_specs=[whole(), whole(), whole()],
        out_specs=(whole(), whole()),
        compiler_params=small(),
        name="finish",
    )(own_sum, returned, logits[None])
    return grad_features, grad_logits[0]


def solution(mesh):
    placed = (
        P(None, ("cam", "space")),
        P(None, ("cam", "space")),
        P(("cam", "space")),
        P(("cam", "space")),
        P(),
        P(),
        P("cam", "space", None, None),
        P("cam", "space", None),
        P("cam", "space", None, None, None),
    )
    return jax.shard_map(
        on_device,
        mesh=mesh,
        in_specs=placed,
        out_specs=(P(None, ("cam", "space")), P(("cam", "space"))),
        check_vma=False,
    )
```

time: 90.1 us -> 71.8 us (0.80)
  the two profiles are of different devices: /device:TPU:24 before, /device:TPU:14 now
where the time goes in v2:
time: 71.8 us; the launch traced here: 71 us
  Pallas kernels  32.3 us (45%)
  starting transfers between devices  25.1 us (35%)
  waiting for transfers between devices  7.57 us (11%)
  local copies, waits for them, and re-layouts  3.83 us (5%)
  other arithmetic  1.51 us (2%)
    pallas_call x1, Pallas kernels, on_device(): pl.pallas_call(forward_kernel, out_shape=tuple((shape((views,) + size, ki...  10.4 us
    pallas_call x1, Pallas kernels, on_device(): pl.pallas_call(backward_kernel, out_shape=(shape((channels + 8, length),...  10.3 us
    ppermute x2, starting transfers between devices, shifted(): return lax.ppermute(shard, axis, pairs)  8.54 us
    all_to_all x1, starting transfers between devices, on_device(): codes = lax.all_to_all(coded, 'cam', 0, 0, tiled=True)  8.47 us
    all_to_all x1, starting transfers between devices, on_device(): received = lax.all_to_all(packed, 'cam', 0, 0, tiled=True)  8.13 us
    pallas_call x1, Pallas kernels, on_device(): pl.pallas_call(pack_kernel, out_shape=shape((tiles, channels + 8, length)...  7.21 us
    ppermute x2, waiting for transfers between devices, shifted(): return lax.ppermute(shard, axis, pairs)  5.84 us
    unnamed x19, local copies, waits for them, and re-layouts  3.83 us
  transfers between devices with their start and end apart: 4, of which 3 were waited for; matrix products, arithmetic and copies ran while one was open for 3% of the time, Pallas kernels for 28%

profile of v2, /device:TPU:14, one launch (start us, length us, event | category | flops | bytes accessed | tf_op | source)
XLA Modules:
  0.0 71.0 jit_solution(3127339494208228634)
XLA Ops:
  0.6 0.0 copy-start.8
  0.6 0.0 copy-start.1
  0.7 0.7 %copy-done.1 = s32[1,1,16,256]{3,2,1,0:T(8,128)S(1)} copy-done((s32[1,1,16,256]{3,2,1,0:T(8,128)S(1)}, s32[1,1,16,256]{3,2,1,0:T(8,128)}, u32[]{:S(2)}) %copy-start.1) | copy-done | bytes 16408
  1.4 0.0 copy-start.3
  1.4 0.7 copy-done.3
  2.0 1.3 %lists.1 = s16[16,8,256]{2,1,0:T(8,128)(2,1)} custom-call(s32[16,256]{1,0:T(8,128)S(1)} %bitcast.9, s32[16]{0:T(128)S(1)} %bitcast.12), custom_call_target="tpu_custom_call" | custom-call | flops 1000000 | bytes 100000 | tf_op jit(solution)/shard_map/lists/pallas_call | solution.py:310
  3.4 8.5 %all-to-all-start.1 = ((s16[16,8,256]{2,1,0:T(8,128)(2,1)}), s16[16,8,256]{2,1,0:T(8,128)(2,1)S(1)}, u32[]{:S(2)}, u32[]{:S(2)}) async-start(s16[16,8,256]{2,1,0:T(8,128)(2,1)} %lists.1), calls=%async_computation.1 | async-start | bytes 131072 | tf_op jit(solution)/shard_map/all_to_all | solution.py:319
  11.8 0.9 %pad_maximum_fusion.own_ref = f32[69,256]{1,0:T(8,128)S(1)} fusion(f32[1,256]{1,0:T(1,128)} %bitcast.10, f32[1,256]{1,0:T(1,128)} %bitcast.14, f32[3,256]{1,0:T(4,128)} %param.10, f32[64,256]{1,0:T(8,128)} %param.9), kind=kLoop, calls=%fused_computation | loop fusion | flops 52992 | bytes 141312 | tf_op jit(solution)/shard_map/concatenate | solution.py:320
  12.7 0.0 copy-start.5
  12.7 1.9 %collective-permute-start = (f32[69,256]{1,0:T(8,128)S(1)}, f32[69,256]{1,0:T(8,128)S(1)}, u32[]{:S(2)}, u32[]{:S(2)}) collective-permute-start(f32[69,256]{1,0:T(8,128)S(1)} %pad_maximum_fusion.own_ref), channel_id=1, source_target_pairs={{0,1},{1,2},{2,3},{3,4},{4,5},{5,6},{6,7},{7,8},{8,9},{9,10},{10,1... | collective-permute-start | bytes 211976 | tf_op jit(solution)/shard_map/ppermute | solution.py:25
  14.7 7.2 %pack.1 = s16[16,72,256]{2,1,0:T(8,128)(2,1)} custom-call(bf16[64,512]{1,0:T(8,128)(2,1)} %decoder_ref.3, bf16[16,256,512]{2,1,0:T(8,128)(2,1)} %bitcast.13), custom_call_target="tpu_custom_call" | custom-call | flops 268435456 | bytes 4718592 | tf_op jit(solution)/shard_map/pack/pallas_call | solution.py:323
  21.9 3.6 %collective-permute-done.upper_ref = f32[69,256]{1,0:T(8,128)S(1)} collective-permute-done((f32[69,256]{1,0:T(8,128)S(1)}, f32[69,256]{1,0:T(8,128)S(1)}, u32[]{:S(2)}, u32[]{:S(2)}) %collective-permute-start) | collective-permute-done | bytes 70688 | tf_op jit(solution)/shard_map/ppermute | solution.py:25
  25.4 0.0 all-to-all-done.1.codes_ref
  25.4 0.0 copy-start.6
  25.4 8.1 %all-to-all-start = ((s16[16,72,256]{2,1,0:T(8,128)(2,1)}), s16[16,72,256]{2,1,0:T(8,128)(2,1)S(1)}, u32[]{:S(2)}, u32[]{:S(2)}) async-start(s16[16,72,256]{2,1,0:T(8,128)(2,1)} %pack.1), calls=%async_computation | async-start | bytes 1179648 | tf_op jit(solution)/shard_map/all_to_all | solution.py:337
  33.6 0.0 copy-done.8
  33.6 0.7 copy.11.camera_ref
  34.3 0.6 pad_maximum_fusion.1.place_ref
  34.9 0.0 copy-done.5
  34.9 0.0 copy-done.7
  34.9 2.4 %prep.1 = (bf16[64,512]{1,0:T(8,128)(2,1)}, bf16[16,16,512]{2,1,0:T(8,128)(2,1)}) custom-call(f32[16,3]{1,0:T(8,128)} %copy.11.camera_ref, f32[3]{0:T(128)} %pad_maximum_fusion.1.place_ref, f32[69,256]{1,0:T(8,128)} %copy-done.5, f32[69,256]{1,0:T(8,128)} %copy-done.7), custom_call_target="tpu_custom_call" | custom-call | flops 10000000 | bytes 1000000 | tf_op jit(solution)/shard_map/prep/pallas_call | solution.py:346
  37.2 0.0 copy-done.6
  37.2 10.4 %forward.1 = (bf16[16,256,80]{2,1,0:T(8,128)(2,1)}, f32[16,256,256]{2,1,0:T(8,128)}, f32[16,256,256]{2,1,0:T(8,128)}, bf16[16,256,256]{2,1,0:T(8,128)(2,1)}, f32...) custom-call(s16[16,8,256]{2,1,0:T(8,128)(2,1)} %copy-done.6, bf16[16,16,512]{2,1,0:T(8,128)(2,1)} %get-tuple-element.18.terms_ref, ...), custom_call_target="tpu_custom_call" | custom-call | flops 1258291200 | bytes 11534336 | tf_op jit(solution)/shard_map/forward/pallas_call | solution.py:369
  47.6 1.7 %all-to-all-done.packed_ref = s16[16,72,256]{2,1,0:T(8,128)(2,1)S(1)} async-done(((s16[16,72,256]{2,1,0:T(8,128)(2,1)}), s16[16,72,256]{2,1,0:T(8,128)(2,1)S(1)}, u32[]{:S(2)}, u32[]{:S(2)}) %all-to-all-start) | async-done | bytes 589856 | tf_op jit(solution)/shard_map/all_to_all | solution.py:337
  49.4 0.0 copy-start.4
  49.4 0.9 %copy-done.4 = s16[16,72,256]{2,1,0:T(8,128)(2,1)} copy-done((s16[16,72,256]{2,1,0:T(8,128)(2,1)}, s16[16,72,256]{2,1,0:T(8,128)(2,1)S(1)}, u32[]{:S(2)}) %copy-start.4) | copy-done | bytes 589848
  50.3 10.3 %backward.1 = (f32[72,256]{1,0:T(8,128)}, f32[72,256]{1,0:T(8,128)}) custom-call(s16[16,72,256]{2,1,0:T(8,128)(2,1)} %copy-done.4, s16[16,8,256]{2,1,0:T(8,128)(2,1)} %copy-done.6, bf16[16,256,80]{2,1,0:T(8,128)(2,1)} %get-tuple-element.20.entry_ref, f32[16,256,256]{2,1,0:T(8,128)} %get-tuple-element.21.a_ref, f32[16,256,256]{2,1,0:T(8,128)} %get-tuple-element.22.w_ref, ...), custom_call_target="tpu_custom_call" | custom-call | flops 1258291200 | bytes 11534336 | tf_op jit(solution)/shard_map/backward/pallas_call | solution.py:394
  60.6 6.6 %collective-permute-start.1 = (f32[72,256]{1,0:T(8,128)}, f32[72,256]{1,0:T(8,128)S(1)}, u32[]{:S(2)}, u32[]{:S(2)}) collective-permute-start(f32[72,256]{1,0:T(8,128)} %get-tuple-element.27), channel_id=1, source_target_pairs={{1,0},{2,1},{3,2},{4,3},{5,4},{6,5},{7,6},{8,7},{9,8},{10,9},{11,1... | collective-permute-start | bytes 221192 | tf_op jit(solution)/shard_map/ppermute | solution.py:25
  67.2 2.3 %collective-permute-done.1.returned_ref = f32[72,256]{1,0:T(8,128)S(1)} collective-permute-done((f32[72,256]{1,0:T(8,128)}, f32[72,256]{1,0:T(8,128)S(1)}, u32[]{:S(2)}, u32[]{:S(2)}) %collective-permute-start.1) | collective-permute-done | bytes 73760 | tf_op jit(solution)/shard_map/ppermute | solution.py:25
  69.5 0.0 copy-done.2
  69.5 0.9 %copy-done = f32[72,256]{1,0:T(8,128)S(1)} copy-done((f32[72,256]{1,0:T(8,128)S(1)}, f32[72,256]{1,0:T(8,128)}, u32[]{:S(2)}) %copy-start) | copy-done | bytes 73752
  70.4 0.6 finish.1
  (3 shorter events, 0.0 us)
Async XLA Ops:
  0.6 32.9 %copy-start.8 = (f32[16,3]{0,1:T(4,128)S(1)}, f32[16,3]{0,1:T(4,128)}, u32[]{:S(2)}) copy-start(f32[16,3]{0,1:T(4,128)} %param.13) | copy-start | bytes 580
  0.6 0.7 %copy-start.1 = (s32[1,1,16,256]{3,2,1,0:T(8,128)S(1)}, s32[1,1,16,256]{3,2,1,0:T(8,128)}, u32[]{:S(2)}) copy-start(s32[1,1,16,256]{3,2,1,0:T(8,128)} %param.15) | copy-start | bytes 49156
  1.4 0.7 copy-start.3
  3.4 22.1 %all-to-all-start.1 = ((s16[16,8,256]{2,1,0:T(8,128)(2,1)}), s16[16,8,256]{2,1,0:T(8,128)(2,1)S(1)}, u32[]{:S(2)}, u32[]{:S(2)}) async-start(s16[16,8,256]{2,1,0:T(8,128)(2,1)} %lists.1), calls=%async_computation.1 | async-start | bytes 131072 | tf_op jit(solution)/shard_map/all_to_all | solution.py:319
  12.7 22.1 %copy-start.5 = (f32[69,256]{1,0:T(8,128)}, f32[69,256]{1,0:T(8,128)S(1)}, u32[]{:S(2)}) copy-start(f32[69,256]{1,0:T(8,128)S(1)} %pad_maximum_fusion.own_ref) | copy-start | bytes 211972
  12.7 12.7 %collective-permute-start = (f32[69,256]{1,0:T(8,128)S(1)}, f32[69,256]{1,0:T(8,128)S(1)}, u32[]{:S(2)}, u32[]{:S(2)}) collective-permute-start(f32[69,256]{1,0:T(8,128)S(1)} %pad_maximum_fusion.own_ref), channel_id=1, source_target_pairs={{0,1},{1,2},{2,3},{3,4},{4,5},{5,6},{6,7},{7,8},{8,9},{9,10},{10,1... | collective-permute-start | bytes 211976 | tf_op jit(solution)/shard_map/ppermute | solution.py:25
  25.4 9.4 %copy-start.7 = (f32[69,256]{1,0:T(8,128)}, f32[69,256]{1,0:T(8,128)S(1)}, u32[]{:S(2)}) copy-start(f32[69,256]{1,0:T(8,128)S(1)} %collective-permute-done.upper_ref) | copy-start | bytes 211972
  25.4 11.8 %copy-start.6 = (s16[16,8,256]{2,1,0:T(8,128)(2,1)}, s16[16,8,256]{2,1,0:T(8,128)(2,1)S(1)}, u32[]{:S(2)}) copy-start(s16[16,8,256]{2,1,0:T(8,128)(2,1)S(1)} %all-to-all-done.1.codes_ref) | copy-start | bytes 196612
  25.4 23.9 %all-to-all-start = ((s16[16,72,256]{2,1,0:T(8,128)(2,1)}), s16[16,72,256]{2,1,0:T(8,128)(2,1)S(1)}, u32[]{:S(2)}, u32[]{:S(2)}) async-start(s16[16,72,256]{2,1,0:T(8,128)(2,1)} %pack.1), calls=%async_computation | async-start | bytes 1179648 | tf_op jit(solution)/shard_map/all_to_all | solution.py:337
  49.4 0.9 %copy-start.4 = (s16[16,72,256]{2,1,0:T(8,128)(2,1)}, s16[16,72,256]{2,1,0:T(8,128)(2,1)S(1)}, u32[]{:S(2)}) copy-start(s16[16,72,256]{2,1,0:T(8,128)(2,1)S(1)} %all-to-all-done.packed_ref) | copy-start | bytes 1769476
  50.3 19.2 %copy-start.2 = (f32[256]{0:T(256)S(1)}, f32[256]{0:T(256)}, u32[]{:S(2)}) copy-start(f32[256]{0:T(256)} %param.12) | copy-start | bytes 3076
  60.6 8.9 %collective-permute-start.1 = (f32[72,256]{1,0:T(8,128)}, f32[72,256]{1,0:T(8,128)S(1)}, u32[]{:S(2)}, u32[]{:S(2)}) collective-permute-start(f32[72,256]{1,0:T(8,128)} %get-tuple-element.27), channel_id=1, source_target_pairs={{1,0},{2,1},{3,2},{4,3},{5,4},{6,5},{7,6},{8,7},{9,8},{10,9},{11,1... | collective-permute-start | bytes 221192 | tf_op jit(solution)/shard_map/ppermute | solution.py:25
  69.5 0.9 %copy-start = (f32[72,256]{1,0:T(8,128)S(1)}, f32[72,256]{1,0:T(8,128)}, u32[]{:S(2)}) copy-start(f32[72,256]{1,0:T(8,128)} %get-tuple-element.26.own_ref) | copy-start | bytes 221188

commit v3 on v2

--- a/solution.py
+++ b/solution.py
@@ -54,16 +54,39 @@
         out_ref[tile] = jnp.broadcast_to(codes[tile : tile + 1, :], (8, length)).astype(jnp.int16)
 
 
-def pack_kernel(decoder_ref, targets_ref, out_ref):
+def pack_kernel(decoder_ref, targets_ref, out_ref, held_ref, built_ref, in_sem, out_sem):
     channels = decoder_ref.shape[0]
-    for turn in range(targets_ref.shape[0]):
-        value = dot(targets_ref[turn], decoder_ref[...], NT).T
-        largest = jnp.max(jnp.abs(value), axis=0, keepdims=True)
-        power = jnp.floor(jnp.log2(jnp.maximum(largest, 1e-30))) + 1.0
-        fixed = jnp.round(value * (FULL * jnp.exp2(-power)))
-        out_ref[turn, 0:channels, :] = fixed.astype(jnp.int32).astype(jnp.int16)
-        powers = jnp.broadcast_to(power, (8, value.shape[1]))
-        out_ref[turn, channels : channels + 8, :] = powers.astype(jnp.int32).astype(jnp.int16)
+    tiles = held_ref.shape[0]
+    group = tiles // out_sem.shape[0]
+
+    def incoming(tile):
+        return pltpu.make_async_copy(targets_ref.at[tile], held_ref.at[tile], in_sem.at[tile])
+
+    def outgoing(turn):
+        span = pl.ds(turn * group, group)
+        return pltpu.make_async_copy(built_ref.at[span], out_ref.at[span], out_sem.at[turn])
+
+    for tile in range(tiles):
+        incoming(tile).start()
+
+    def build(turn, carry):
+        for step in range(group):
+            incoming(turn * group + step).wait()
+        for step in range(group):
+            tile = turn * group + step
+            value = dot(held_ref[tile], decoder_ref[...], NT).T
+            largest = jnp.max(jnp.abs(value), axis=0, keepdims=True)
+            power = jnp.floor(jnp.log2(jnp.maximum(largest, 1e-30))) + 1.0
+            fixed_point = jnp.round(value * (FULL * jnp.exp2(-power)))
+            built_ref[tile, 0:channels, :] = fixed_point.astype(jnp.int32).astype(jnp.int16)
+            powers = jnp.broadcast_to(power, (8, value.shape[1]))
+            built_ref[tile, channels : channels + 8, :] = powers.astype(jnp.int32).astype(jnp.int16)
+        outgoing(turn).start()
+        return carry
+
+    lax.fori_loop(0, out_sem.shape[0], build, 0)
+    for turn in range(out_sem.shape[0]):
+        outgoing(turn).wait()
 
 
 def prep_kernel(camera_ref, place_ref, own_ref, upper_ref, feature_ref, terms_ref, row_ref):
@@ -101,10 +124,13 @@
     return jnp.where(inside, moved, fill)
 
 
-def in_turns(works):
-    works = list(works)
+def in_turns(works, before=()):
+    works, stage = list(works), 0
     while works:
+        if stage < len(before):
+            before[stage]()
         works = [work for work in works if next(work, None) is not None]
+        stage += 1
 
 
 def hot_rows(wanted_ref, codes, hot_ref):
@@ -159,9 +185,12 @@
     ends_ref[0:8, :] = start
     ends_ref[8:16, :] = keep
     yield True
+    both = jnp.concatenate([start, start], axis=0)
     for i in range(steps // 2):
         rows = pl.ds(16 * i, 16)
-        wb_ref[rows, :] = (w_ref[rows, :] * jnp.concatenate([start, start], axis=0)).astype(BF16)
+        weight = w_ref[rows, :] * both
+        w_ref[rows, :] = weight
+        wb_ref[rows, :] = weight.astype(BF16)
     yield True
     composite = dot(feature_t, wb_ref[...], NN).astype(BF16)
     projected_ref[...] = dot(squares_ref[...], jnp.concatenate([composite] * 3, axis=0), NN)
@@ -198,25 +227,29 @@
 
 
 def backward_tile(
-    packed_ref, codes_ref, entry_ref, a_ref, w_ref, wb_ref, ends_ref, projected_ref, wanted_ref,
+    codes_ref, packed_ref, projected_ref, entry_ref, w_ref, ends_ref, a_ref, wb_ref, wanted_ref,
     own_ref, upper_ref, hot_ref, ct_ref, ts_ref
 ):
     channels, length = projected_ref.shape
     steps = length // 8
     index = lax.broadcasted_iota(jnp.int32, (8, length), 0)
+    hot_rows(wanted_ref, codes_ref[...].astype(jnp.int32).astype(F32), hot_ref)
+    yield True
     packed = packed_ref[...].astype(jnp.int32).astype(F32)
     scale = jnp.exp2(packed[channels : channels + 1, :]) * (1.0 / FULL)
     pixel_grad = (projected_ref[...] - packed[0:channels] * scale).astype(BF16)
     padded = jnp.concatenate([pixel_grad, jnp.zeros((16, length), BF16)], axis=0)
     yield True
+    for first in range(0, length, 64):
+        ct_ref[first : first + 64, :] = dot(entry_ref[first : first + 64, :], padded, NN)
+    yield True
     total = jnp.zeros((8, length), F32)
-    for first in range(0, length, 64):
-        ct = dot(entry_ref[first : first + 64, :], padded, NN)
-        ct_ref[first : first + 64, :] = ct
-        for i in range(8):
-            total = total + w_ref[pl.ds(first + 8 * i, 8), :] * ct[8 * i : 8 * i + 8, :]
+    for i in range(steps):
+        rows = pl.ds(8 * i, 8)
+        total = total + w_ref[rows, :] * ct_ref[rows, :]
     yield True
     start, factor = ends_ref[0:8, :], ends_ref[8:16, :]
+    total = jnp.where(start > 0.0, total / start, 0.0)
     for by in (1, 2, 4):
         total = total + factor * shift_rows(total, -by, 0.0, index)
         factor = factor * shift_rows(factor, -by, 1.0, index)
@@ -224,18 +257,13 @@
     for i in reversed(range(steps)):
         rows = pl.ds(8 * i, 8)
         gap = ct_ref[rows, :] - after
-        term = (w_ref[rows, :] * start) * gap
+        term = w_ref[rows, :] * gap
         after = after + a_ref[rows, :] * gap
         ts_ref[rows, :] = term[:, 0:128] + term[:, 128:256]
     yield True
     feature_grad = dot(pixel_grad, wb_ref[...], NT)
-    hot_rows(wanted_ref, codes_ref[...].astype(jnp.int32).astype(F32), hot_ref)
-    yield True
-    sums = ts_ref[...]
-    sums_hi = sums.astype(BF16)
-    sums_lo = (sums - sums_hi.astype(F32)).astype(BF16)
-    ones = jnp.ones((8, length), BF16)
-    logit_row = dot(ones, jnp.concatenate([sums_hi, sums_lo], axis=1), NT)
+    yield True
+    logit_row = jnp.broadcast_to(jnp.sum(ts_ref[...].T, axis=0, keepdims=True), (8, length))
     grad_hi = feature_grad.astype(BF16)
     grad_lo = (feature_grad - grad_hi.astype(F32)).astype(BF16)
     logit_hi = logit_row.astype(BF16).astype(F32)
@@ -250,26 +278,50 @@
         ref[c : c + 8, :] += part[2 * c : 2 * c + 8] + part[2 * c + 8 : 2 * c + 16]
 
 
-def backward_kernel(
-    packed_ref, codes_ref, entry_ref, a_ref, w_ref, wb_ref, ends_ref, projected_ref,
-    own_ref, upper_ref, wanted_ref, hot_ref, ct_ref, ts_ref
-):
-    @pl.when(pl.program_id(0) == 0)
-    def _():
-        set_wanted(wanted_ref)
-        own_ref[...] = jnp.zeros(own_ref.shape, F32)
-        upper_ref[...] = jnp.zeros(upper_ref.shape, F32)
-
-    in_turns(
-        backward_tile(
-            *(
-                ref.at[turn]
-                for ref in (packed_ref, codes_ref, entry_ref, a_ref, w_ref, wb_ref, ends_ref, projected_ref)
+def backward_kernel(*refs):
+    count = (len(refs) - 7) // 2
+    sources, (own_ref, upper_ref) = refs[:count], refs[count : count + 2]
+    held = refs[count + 2 : 2 * count + 2]
+    wanted_ref, hot_ref, ct_ref, ts_ref, sem = refs[2 * count + 2 :]
+    group, turns = hot_ref.shape[0], sem.shape[0]
+
+    def copies(turn):
+        span = pl.ds(turn * group, group)
+        return [
+            pltpu.make_async_copy(source.at[span], place.at[span], sem.at[turn, index])
+            for index, (source, place) in enumerate(zip(sources, held))
+        ]
+
+    for turn in range(turns):
+        for copy in copies(turn):
+            copy.start()
+    set_wanted(wanted_ref)
+    own_ref[...] = jnp.zeros(own_ref.shape, F32)
+    upper_ref[...] = jnp.zeros(upper_ref.shape, F32)
+
+    def build(turn, carry):
+        pending = copies(turn)
+
+        def arrived(first, last):
+            def wait():
+                for copy in pending[first:last]:
+                    copy.wait()
+
+            return wait
+
+        in_turns(
+            (
+                backward_tile(
+                    *(ref.at[turn * group + step] for ref in held),
+                    wanted_ref, own_ref, upper_ref, hot_ref.at[step], ct_ref.at[step], ts_ref.at[step],
+                )
+                for step in range(group)
             ),
-            wanted_ref, own_ref, upper_ref, hot_ref.at[turn], ct_ref.at[turn], ts_ref.at[turn],
+            (arrived(0, 1), arrived(1, 8)),
         )
-        for turn in range(hot_ref.shape[0])
-    )
+        return carry
+
+    lax.fori_loop(0, turns, build, 0)
 
 
 def finish_kernel(own_ref, returned_ref, logits_ref, feature_ref, logit_ref):
@@ -295,70 +347,8 @@
     return pl.BlockSpec(shape, lambda t: (0,) * len(shape))
 
 
-def on_device(features, positions, spreads, logits, camera, decoder, tile_lists, counts, targets):
-    channels, length = features.shape
-    tiles = tile_lists.shape[2]
-    decoded = decoder.shape[1]
-    views = camera.shape[0]
-    pack_group, group = 2, 2
-    column = lax.axis_index("cam")
-    tile_row = lax.axis_index("space")
-    image_width = TS * lax.axis_size("cam")
-    image_height = TS * lax.axis_size("space")
-    shape = jax.ShapeDtypeStruct
-
-    coded = pl.pallas_call(
-        list_kernel,
-        out_shape=shape((tiles, 8, length), jnp.int16),
-        in_specs=[whole(), pl.BlockSpec(memory_space=pltpu.SMEM)],
-        out_specs=whole(),
-        compiler_params=small(),
-        cost_estimate=pl.CostEstimate(flops=1000000, bytes_accessed=100000, transcendentals=0),
-        name="lists",
-    )(tile_lists[0, 0], counts[0, 0])
-    codes = lax.all_to_all(coded, "cam", 0, 0, tiled=True)
-    own_slab = jnp.concatenate([features, positions, spreads[None], logits[None]], axis=0)
-    upper_slab = shifted(own_slab, "space", 1)
-
-    packed = pl.pallas_call(
-        pack_kernel,
-        out_shape=shape((tiles, channels + 8, length), jnp.int16),
-        grid=(tiles // pack_group,),
-        in_specs=[fixed(channels, decoded), blocks(pack_group, length, decoded)],
-        out_specs=blocks(pack_group, channels + 8, length),
-        cost_estimate=pl.CostEstimate(
-            flops=2 * tiles * length * channels * decoded,
-            bytes_accessed=tiles * length * (2 * decoded + 2 * channels),
-            transcendentals=0,
-        ),
-        name="pack",
-    )(decoder, targets[0, 0])
-    packed, upper_slab = lax.optimization_barrier((packed, upper_slab))
-    received = lax.all_to_all(packed, "cam", 0, 0, tiled=True)
-
-    place = jnp.stack(
-        [
-            0.5 * image_width - (column * TS + 0.5 * TS),
-            0.5 * image_height - (tile_row * TS + 0.5 * TS),
-            tile_row,
-        ]
-    ).astype(F32)
-    feature_bf, terms = pl.pallas_call(
-        prep_kernel,
-        out_shape=(shape((channels, 2 * length), BF16), shape((views, 16, 2 * length), BF16)),
-        in_specs=[
-            pl.BlockSpec(memory_space=pltpu.SMEM),
-            pl.BlockSpec(memory_space=pltpu.SMEM),
-            whole(),
-            whole(),
-        ],
-        out_specs=(whole(), whole()),
-        scratch_shapes=[pltpu.VMEM((16, 2 * length), F32)],
-        cost_estimate=pl.CostEstimate(flops=10000000, bytes_accessed=1000000, transcendentals=20000),
-        name="prep",
-    )(camera, place, own_slab, upper_slab)
-
-    kept = (
+def kept_sizes(channels, length):
+    return (
         ((length, channels + 16), BF16),
         ((length, length), F32),
         ((length, length), F32),
@@ -366,7 +356,14 @@
         ((16, length), F32),
         ((channels, length), F32),
     )
-    saved = pl.pallas_call(
+
+
+def forward(codes, terms, feature_bf, decoder, group=4):
+    channels, decoded = decoder.shape
+    views, length = codes.shape[0], codes.shape[2]
+    shape = jax.ShapeDtypeStruct
+    kept = kept_sizes(channels, length)
+    return pl.pallas_call(
         forward_kernel,
         out_shape=tuple(shape((views,) + size, kind) for size, kind in kept),
         grid=(views // group,),
@@ -391,21 +388,25 @@
         name="forward",
     )(codes, terms, feature_bf, decoder)
 
-    own_sum, upper_sum = pl.pallas_call(
+
+def backward(received, codes, saved, group=4):
+    channels = saved[-1].shape[1]
+    views, length = codes.shape[0], codes.shape[2]
+    shape = jax.ShapeDtypeStruct
+    entry, a, w, wb, ends, projected = saved
+    operands = (codes, received, projected, entry, w, ends, a, wb)
+    return pl.pallas_call(
         backward_kernel,
         out_shape=(shape((channels + 8, length), F32),) * 2,
-        grid=(views // group,),
-        in_specs=[
-            blocks(group, channels + 8, length),
-            blocks(group, 8, length),
-            *(blocks(group, *size) for size, _ in kept),
-        ],
+        in_specs=[pl.BlockSpec(memory_space=pl.ANY)] * len(operands),
         out_specs=(whole(),) * 2,
         scratch_shapes=[
+            *(pltpu.VMEM(operand.shape, operand.dtype) for operand in operands),
             pltpu.VMEM((2 * length, 128), BF16),
             pltpu.VMEM((group, 2 * length, length), BF16),
             pltpu.VMEM((group, length, length), F32),
             pltpu.VMEM((group, length, 128), F32),
+            pltpu.SemaphoreType.DMA((views // group, len(operands))),
         ],
         cost_estimate=pl.CostEstimate(
             flops=views * 2 * length * length * 600,
@@ -413,7 +414,84 @@
             transcendentals=0,
         ),
         name="backward",
-    )(received, codes, *saved)
+    )(*operands)
+
+
+def pack(decoder, targets, group=4):
+    channels = decoder.shape[0]
+    tiles, length, decoded = targets.shape
+    shape = (tiles, channels + 8, length)
+    return pl.pallas_call(
+        pack_kernel,
+        out_shape=jax.ShapeDtypeStruct(shape, jnp.int16),
+        in_specs=[whole(), pl.BlockSpec(memory_space=pl.ANY)],
+        out_specs=pl.BlockSpec(memory_space=pl.ANY),
+        scratch_shapes=[
+            pltpu.VMEM(targets.shape, BF16),
+            pltpu.VMEM(shape, jnp.int16),
+            pltpu.SemaphoreType.DMA((tiles,)),
+            pltpu.SemaphoreType.DMA((tiles // group,)),
+        ],
+        cost_estimate=pl.CostEstimate(
+            flops=2 * tiles * length * channels * decoded,
+            bytes_accessed=tiles * length * (2 * decoded + 2 * channels),
+            transcendentals=0,
+        ),
+        name="pack",
+    )(decoder, targets)
+
+
+def on_device(features, positions, spreads, logits, camera, decoder, tile_lists, counts, targets):
+    channels, length = features.shape
+    tiles = tile_lists.shape[2]
+    views = camera.shape[0]
+    column = lax.axis_index("cam")
+    tile_row = lax.axis_index("space")
+    image_width = TS * lax.axis_size("cam")
+    image_height = TS * lax.axis_size("space")
+    shape = jax.ShapeDtypeStruct
+
+    coded = pl.pallas_call(
+        list_kernel,
+        out_shape=shape((tiles, 8, length), jnp.int16),
+        in_specs=[whole(), pl.BlockSpec(memory_space=pltpu.SMEM)],
+        out_specs=whole(),
+        compiler_params=small(),
+        cost_estimate=pl.CostEstimate(flops=1000000, bytes_accessed=100000, transcendentals=0),
+        name="lists",
+    )(tile_lists[0, 0], counts[0, 0])
+    codes = lax.all_to_all(coded, "cam", 0, 0, tiled=True)
+    own_slab = jnp.concatenate([features, positions, spreads[None], logits[None]], axis=0)
+    upper_slab = shifted(own_slab, "space", 1)
+
+    packed = pack(decoder, targets[0, 0])
+    packed, upper_slab = lax.optimization_barrier((packed, upper_slab))
+    received = lax.all_to_all(packed, "cam", 0, 0, tiled=True)
+
+    place = jnp.stack(
+        [
+            0.5 * image_width - (column * TS + 0.5 * TS),
+            0.5 * image_height - (tile_row * TS + 0.5 * TS),
+            tile_row,
+        ]
+    ).astype(F32)
+    feature_bf, terms = pl.pallas_call(
+        prep_kernel,
+        out_shape=(shape((channels, 2 * length), BF16), shape((views, 16, 2 * length), BF16)),
+        in_specs=[
+            pl.BlockSpec(memory_space=pltpu.SMEM),
+            pl.BlockSpec(memory_space=pltpu.SMEM),
+            whole(),
+            whole(),
+        ],
+        out_specs=(whole(), whole()),
+        scratch_shapes=[pltpu.VMEM((16, 2 * length), F32)],
+        cost_estimate=pl.CostEstimate(flops=10000000, bytes_accessed=1000000, transcendentals=20000),
+        name="prep",
+    )(camera, place, own_slab, upper_slab)
+
+    saved = forward(codes, terms, feature_bf, decoder)
+    own_sum, upper_sum = backward(received, codes, saved)
     returned = shifted(upper_sum, "space", -1)
     grad_features, grad_logits = pl.pallas_call(
         finish_kernel,

time: 71.8 us -> 66.2 us (0.922)
  Pallas kernels: 32.3 us -> 24.9 us
  waiting for transfers between devices: 7.57 us -> 9.52 us
    pallas_call x3, Pallas kernels: 27.9 us -> 20.5 us  [the longest x1 8.49 us: forward(): pl.pallas_call(forward_kernel, out_shape=tuple((shape((views,) + size, ki...]
    ppermute x2, waiting for transfers between devices: 5.84 us -> 8.03 us  [shifted(): return lax.ppermute(shard, axis, pairs)]
  transfers between devices with their start and end apart: 4 -> 4, of which waited for: 3 -> 3; matrix products, arithmetic and copies ran while one was open for 3% -> 3% of each run, Pallas kernels for 28% -> 24%
where the time goes in v3:
time: 66.2 us; the launch traced here: 65.6 us
  starting transfers between devices  25.2 us (38%)
  Pallas kernels  24.9 us (38%)
  waiting for transfers between devices  9.52 us (14%)
  local copies, waits for them, and re-layouts  3.83 us (6%)
  other arithmetic  1.51 us (2%)
  between operations  0.7 us (1%)
    ppermute x2, starting transfers between devices, shifted(): return lax.ppermute(shard, axis, pairs)  8.58 us
    pallas_call x1, Pallas kernels, forward(): pl.pallas_call(forward_kernel, out_shape=tuple((shape((views,) + size, ki...  8.49 us
    all_to_all x1, starting transfers between devices, on_device(): codes = lax.all_to_all(coded, 'cam', 0, 0, tiled=True)  8.47 us
    all_to_all x1, starting transfers between devices, on_device(): received = lax.all_to_all(packed, 'cam', 0, 0, tiled=True)  8.13 us
    ppermute x2, waiting for transfers between devices, shifted(): return lax.ppermute(shard, axis, pairs)  8.03 us
    pallas_call x1, Pallas kernels, backward(): pl.pallas_call(backward_kernel, out_shape=(shape((channels + 8, length),...  7.02 us
    pallas_call x1, Pallas kernels, pack(): pl.pallas_call(pack_kernel, out_shape=jax.ShapeDtypeStruct(shape, jnp.int...  5.01 us
    unnamed x19, local copies, waits for them, and re-layouts  3.83 us
  transfers between devices with their start and end apart: 4, of which 3 were waited for; matrix products, arithmetic and copies ran while one was open for 3% of the time, Pallas kernels for 24%

profile of v3, /device:TPU:14, one launch (start us, length us, event | category | flops | bytes accessed | tf_op | source)
XLA Modules:
  0.0 65.6 jit_solution(7511426564696543419)
XLA Ops:
  0.6 0.0 copy-start.8
  0.6 0.0 copy-start.1
  0.7 0.7 %copy-done.1 = s32[1,1,16,256]{3,2,1,0:T(8,128)S(1)} copy-done((s32[1,1,16,256]{3,2,1,0:T(8,128)S(1)}, s32[1,1,16,256]{3,2,1,0:T(8,128)}, u32[]{:S(2)}) %copy-start.1) | copy-done | bytes 16408
  1.4 0.0 copy-start.3
  1.4 0.7 copy-done.3
  2.0 1.3 %lists.1 = s16[16,8,256]{2,1,0:T(8,128)(2,1)} custom-call(s32[16,256]{1,0:T(8,128)S(1)} %bitcast.9, s32[16]{0:T(128)S(1)} %bitcast.12), custom_call_target="tpu_custom_call" | custom-call | flops 1000000 | bytes 100000 | tf_op jit(solution)/shard_map/lists/pallas_call | solution.py:454
  3.4 8.5 %all-to-all-start = ((s16[16,8,256]{2,1,0:T(8,128)(2,1)}), s16[16,8,256]{2,1,0:T(8,128)(2,1)S(1)}, u32[]{:S(2)}, u32[]{:S(2)}) async-start(s16[16,8,256]{2,1,0:T(8,128)(2,1)} %lists.1), calls=%async_computation | async-start | bytes 131072 | tf_op jit(solution)/shard_map/all_to_all | solution.py:463
  11.8 0.9 %pad_maximum_fusion.own_ref = f32[69,256]{1,0:T(8,128)S(1)} fusion(f32[1,256]{1,0:T(1,128)} %bitcast.10, f32[1,256]{1,0:T(1,128)} %bitcast.14, f32[3,256]{1,0:T(4,128)} %param.10, f32[64,256]{1,0:T(8,128)} %param.9), kind=kLoop, calls=%fused_computation | loop fusion | flops 52992 | bytes 141312 | tf_op jit(solution)/shard_map/concatenate | solution.py:464
  12.7 0.0 copy-start.5
  12.7 1.9 %collective-permute-start = (f32[69,256]{1,0:T(8,128)S(1)}, f32[69,256]{1,0:T(8,128)S(1)}, u32[]{:S(2)}, u32[]{:S(2)}) collective-permute-start(f32[69,256]{1,0:T(8,128)S(1)} %pad_maximum_fusion.own_ref), channel_id=1, source_target_pairs={{0,1},{1,2},{2,3},{3,4},{4,5},{5,6},{6,7},{7,8},{8,9},{9,10},{10,1... | collective-permute-start | bytes 211976 | tf_op jit(solution)/shard_map/ppermute | solution.py:25
  14.7 5.0 %pack.1 = s16[16,72,256]{2,1,0:T(8,128)(2,1)} custom-call(bf16[64,512]{1,0:T(8,128)(2,1)} %decoder_ref.3, bf16[16,256,512]{2,1,0:T(8,128)(2,1)} %bitcast.13), custom_call_target="tpu_custom_call" | custom-call | flops 268435456 | bytes 4718592 | tf_op jit(solution)/shard_map/pack/pallas_call | solution.py:424
  19.7 5.7 %collective-permute-done.upper_ref = f32[69,256]{1,0:T(8,128)S(1)} collective-permute-done((f32[69,256]{1,0:T(8,128)S(1)}, f32[69,256]{1,0:T(8,128)S(1)}, u32[]{:S(2)}, u32[]{:S(2)}) %collective-permute-start) | collective-permute-done | bytes 70688 | tf_op jit(solution)/shard_map/ppermute | solution.py:25
  25.4 0.0 copy-start.7
  25.4 0.0 all-to-all-done.codes_ref.refs_0_
  25.4 0.0 copy-start.6
  25.4 8.1 %all-to-all-start.1 = ((s16[16,72,256]{2,1,0:T(8,128)(2,1)}), s16[16,72,256]{2,1,0:T(8,128)(2,1)S(1)}, u32[]{:S(2)}, u32[]{:S(2)}) async-start(s16[16,72,256]{2,1,0:T(8,128)(2,1)} %pack.1), calls=%async_computation.1 | async-start | bytes 1179648 | tf_op jit(solution)/shard_map/all_to_all | solution.py:469
  33.6 0.0 copy-done.8
  33.6 0.7 %copy.11.camera_ref = f32[16,3]{1,0:T(8,128)} copy(f32[16,3]{0,1:T(4,128)S(1)} %copy-done.8) | data formatting | bytes 384 | tf_op args[4]
  34.3 0.6 pad_maximum_fusion.1.place_ref
  34.9 0.0 copy-done.5
  34.9 0.0 copy-done.7
  34.9 2.4 %prep.1 = (bf16[64,512]{1,0:T(8,128)(2,1)}, bf16[16,16,512]{2,1,0:T(8,128)(2,1)}) custom-call(f32[16,3]{1,0:T(8,128)} %copy.11.camera_ref, f32[3]{0:T(128)} %pad_maximum_fusion.1.place_ref, f32[69,256]{1,0:T(8,128)} %copy-done.5, f32[69,256]{1,0:T(8,128)} %copy-done.7), custom_call_target="tpu_custom_call" | custom-call | flops 10000000 | bytes 1000000 | tf_op jit(solution)/shard_map/prep/pallas_call | solution.py:478
  37.2 0.0 copy-done.6
  37.2 8.5 %forward.1 = (bf16[16,256,80]{2,1,0:T(8,128)(2,1)}, f32[16,256,256]{2,1,0:T(8,128)}, f32[16,256,256]{2,1,0:T(8,128)}, bf16[16,256,256]{2,1,0:T(8,128)(2,1)}, f32...) custom-call(s16[16,8,256]{2,1,0:T(8,128)(2,1)} %copy-done.6, bf16[16,16,512]{2,1,0:T(8,128)(2,1)} %get-tuple-element.18.terms_ref, ...), custom_call_target="tpu_custom_call" | custom-call | flops 1258291200 | bytes 11534336 | tf_op jit(solution)/shard_map/forward/pallas_call | solution.py:366
  45.7 1.5 %all-to-all-done.1.refs_1_ = s16[16,72,256]{2,1,0:T(8,128)(2,1)S(1)} async-done(((s16[16,72,256]{2,1,0:T(8,128)(2,1)}), s16[16,72,256]{2,1,0:T(8,128)(2,1)S(1)}, u32[]{:S(2)}, u32[]{:S(2)}) %all-to-all-start.1) | async-done | bytes 589856 | tf_op jit(solution)/shard_map/all_to_all | solution.py:469
  47.2 0.9 %copy-done.4 = s16[16,72,256]{2,1,0:T(8,128)(2,1)} copy-done((s16[16,72,256]{2,1,0:T(8,128)(2,1)}, s16[16,72,256]{2,1,0:T(8,128)(2,1)S(1)}, u32[]{:S(2)}) %copy-start.4) | copy-done | bytes 589848
  48.1 7.0 %backward.1 = (f32[72,256]{1,0:T(8,128)}, f32[72,256]{1,0:T(8,128)}) custom-call(s16[16,8,256]{2,1,0:T(8,128)(2,1)} %copy-done.6, s16[16,72,256]{2,1,0:T(8,128)(2,1)} %copy-done.4, f32[16,64,256]{2,1,0:T(8,128)} %get-tuple-element.20.refs_2_, bf16[16,256,80]{2,1,0:T(8,128)(2,1)} %get-tuple-element.21.refs_3_, f32[16,256,256]{2,1,0:T(8,128)} %get-tuple-element.22.refs_4_, ...), custom_call_target="tpu_custom_call" | custom-call | flops 1258291200 | bytes 11534336 | tf_op jit(solution)/shard_map/backward/pallas_call | solution.py:398
  55.1 6.7 %collective-permute-start.1 = (f32[72,256]{1,0:T(8,128)}, f32[72,256]{1,0:T(8,128)S(1)}, u32[]{:S(2)}, u32[]{:S(2)}) collective-permute-start(f32[72,256]{1,0:T(8,128)} %get-tuple-element.27), channel_id=1, source_target_pairs={{1,0},{2,1},{3,2},{4,3},{5,4},{6,5},{7,6},{8,7},{9,8},{10,9},{11,1... | collective-permute-start | bytes 221192 | tf_op jit(solution)/shard_map/ppermute | solution.py:25
  61.8 2.3 %collective-permute-done.1.returned_ref = f32[72,256]{1,0:T(8,128)S(1)} collective-permute-done((f32[72,256]{1,0:T(8,128)}, f32[72,256]{1,0:T(8,128)S(1)}, u32[]{:S(2)}, u32[]{:S(2)}) %collective-permute-start.1) | collective-permute-done | bytes 73760 | tf_op jit(solution)/shard_map/ppermute | solution.py:25
  64.1 0.0 copy-done.2
  64.1 0.9 %copy-done = f32[72,256]{1,0:T(8,128)S(1)} copy-done((f32[72,256]{1,0:T(8,128)S(1)}, f32[72,256]{1,0:T(8,128)}, u32[]{:S(2)}) %copy-start) | copy-done | bytes 73752
  64.9 0.6 finish.1
  (3 shorter events, 0.0 us)
Async XLA Ops:
  0.6 32.9 %copy-start.8 = (f32[16,3]{0,1:T(4,128)S(1)}, f32[16,3]{0,1:T(4,128)}, u32[]{:S(2)}) copy-start(f32[16,3]{0,1:T(4,128)} %param.13) | copy-start | bytes 580
  0.6 0.7 %copy-start.1 = (s32[1,1,16,256]{3,2,1,0:T(8,128)S(1)}, s32[1,1,16,256]{3,2,1,0:T(8,128)}, u32[]{:S(2)}) copy-start(s32[1,1,16,256]{3,2,1,0:T(8,128)} %param.15) | copy-start | bytes 49156
  1.4 0.7 copy-start.3
  3.4 22.1 %all-to-all-start = ((s16[16,8,256]{2,1,0:T(8,128)(2,1)}), s16[16,8,256]{2,1,0:T(8,128)(2,1)S(1)}, u32[]{:S(2)}, u32[]{:S(2)}) async-start(s16[16,8,256]{2,1,0:T(8,128)(2,1)} %lists.1), calls=%async_computation | async-start | bytes 131072 | tf_op jit(solution)/shard_map/all_to_all | solution.py:463
  12.7 22.1 %copy-start.5 = (f32[69,256]{1,0:T(8,128)}, f32[69,256]{1,0:T(8,128)S(1)}, u32[]{:S(2)}) copy-start(f32[69,256]{1,0:T(8,128)S(1)} %pad_maximum_fusion.own_ref) | copy-start | bytes 211972
  12.7 12.7 %collective-permute-start = (f32[69,256]{1,0:T(8,128)S(1)}, f32[69,256]{1,0:T(8,128)S(1)}, u32[]{:S(2)}, u32[]{:S(2)}) collective-permute-start(f32[69,256]{1,0:T(8,128)S(1)} %pad_maximum_fusion.own_ref), channel_id=1, source_target_pairs={{0,1},{1,2},{2,3},{3,4},{4,5},{5,6},{6,7},{7,8},{8,9},{9,10},{10,1... | collective-permute-start | bytes 211976 | tf_op jit(solution)/shard_map/ppermute | solution.py:25
  25.4 9.4 %copy-start.7 = (f32[69,256]{1,0:T(8,128)}, f32[69,256]{1,0:T(8,128)S(1)}, u32[]{:S(2)}) copy-start(f32[69,256]{1,0:T(8,128)S(1)} %collective-permute-done.upper_ref) | copy-start | bytes 211972
  25.4 11.8 %copy-start.6 = (s16[16,8,256]{2,1,0:T(8,128)(2,1)}, s16[16,8,256]{2,1,0:T(8,128)(2,1)S(1)}, u32[]{:S(2)}) copy-start(s16[16,8,256]{2,1,0:T(8,128)(2,1)S(1)} %all-to-all-done.codes_ref.refs_0_) | copy-start | bytes 196612
  25.4 21.8 %all-to-all-start.1 = ((s16[16,72,256]{2,1,0:T(8,128)(2,1)}), s16[16,72,256]{2,1,0:T(8,128)(2,1)S(1)}, u32[]{:S(2)}, u32[]{:S(2)}) async-start(s16[16,72,256]{2,1,0:T(8,128)(2,1)} %pack.1), calls=%async_computation.1 | async-start | bytes 1179648 | tf_op jit(solution)/shard_map/all_to_all | solution.py:469
  47.2 0.9 %copy-start.4 = (s16[16,72,256]{2,1,0:T(8,128)(2,1)}, s16[16,72,256]{2,1,0:T(8,128)(2,1)S(1)}, u32[]{:S(2)}) copy-start(s16[16,72,256]{2,1,0:T(8,128)(2,1)S(1)} %all-to-all-done.1.refs_1_) | copy-start | bytes 1769476
  48.1 16.0 %copy-start.2 = (f32[256]{0:T(256)S(1)}, f32[256]{0:T(256)}, u32[]{:S(2)}) copy-start(f32[256]{0:T(256)} %param.12) | copy-start | bytes 3076
  55.1 8.9 %collective-permute-start.1 = (f32[72,256]{1,0:T(8,128)}, f32[72,256]{1,0:T(8,128)S(1)}, u32[]{:S(2)}, u32[]{:S(2)}) collective-permute-start(f32[72,256]{1,0:T(8,128)} %get-tuple-element.27), channel_id=1, source_target_pairs={{1,0},{2,1},{3,2},{4,3},{5,4},{6,5},{7,6},{8,7},{9,8},{10,9},{11,1... | collective-permute-start | bytes 221192 | tf_op jit(solution)/shard_map/ppermute | solution.py:25
  64.1 0.9 %copy-start = (f32[72,256]{1,0:T(8,128)S(1)}, f32[72,256]{1,0:T(8,128)}, u32[]{:S(2)}) copy-start(f32[72,256]{1,0:T(8,128)} %get-tuple-element.26.own_ref) | copy-start | bytes 221188

commit v4 on v3

--- a/solution.py
+++ b/solution.py
@@ -89,33 +89,47 @@
         outgoing(turn).wait()
 
 
-def prep_kernel(camera_ref, place_ref, own_ref, upper_ref, feature_ref, terms_ref, row_ref):
+def prep_kernel(camera_ref, own_ref, upper_ref, feature_ref, terms_ref, row_ref):
     channels, length = feature_ref.shape[0], own_ref.shape[1]
+    views, lines = terms_ref.shape[0], terms_ref.shape[1]
+    column = lax.axis_index("cam").astype(F32)
+    tile_row = lax.axis_index("space")
+    band = tile_row.astype(F32)
     feature_ref[:, 0:length] = own_ref[0:channels, :].astype(BF16)
     feature_ref[:, length:] = upper_ref[0:channels, :].astype(BF16)
 
     def both(row):
         own = own_ref[row : row + 1, :]
-        return jnp.concatenate([own, jnp.where(place_ref[2] > 0.0, upper_ref[row : row + 1, :], own)], axis=1)
+        upper = jnp.where(tile_row > 0, upper_ref[row : row + 1, :], own)
+        return jnp.broadcast_to(jnp.concatenate([own, upper], axis=1), (views, 2 * length))
+
+    def viewer(part):
+        index = lax.broadcasted_iota(jnp.int32, (views, 128), 0)
+        value = jnp.zeros((views, 128), F32)
+        for view in range(views):
+            value = jnp.where(index == view, camera_ref[part, view], value)
+        return jnp.concatenate([value] * (2 * length // 128), axis=1)
 
     place_x, place_y, depth, spread, logit = (both(channels + i) for i in range(5))
     log_open = LOG2E * (
         jnp.log(0.99) - (jnp.maximum(-logit, 0.0) + jnp.log(1.0 + jnp.exp(-jnp.abs(logit))))
     )
-    row_ref[...] = jnp.zeros(row_ref.shape, F32)
-    centre_u, centre_v = place_ref[0], place_ref[1]
-    for view in range(terms_ref.shape[0]):
-        distance = depth - 0.05 * camera_ref[view, 2]
-        u = (place_x - 0.75 * TS * camera_ref[view, 0]) / distance + centre_u
-        v = (place_y - 0.75 * TS * camera_ref[view, 1]) / distance + centre_v
-        radius = spread / distance
-        inverse = (0.5 * LOG2E) / (radius * radius)
-        terms = (log_open - inverse * (u * u + v * v), 2.0 * inverse * u, 2.0 * inverse * v, -inverse)
-        for index, term in enumerate(terms):
-            for turn, piece in enumerate(pieces(term)):
-                at = 3 * index + turn
-                row_ref[at : at + 1, :] = piece
-        terms_ref[view] = row_ref[...].astype(BF16)
+    distance = depth - 0.05 * viewer(2)
+    u = (place_x - 0.75 * TS * viewer(0)) / distance
+    v = (place_y - 0.75 * TS * viewer(1)) / distance
+    u = u + (0.5 * TS * lax.axis_size("cam") - (column * TS + 0.5 * TS))
+    v = v + (0.5 * TS * lax.axis_size("space") - (band * TS + 0.5 * TS))
+    radius = spread / distance
+    inverse = (0.5 * LOG2E) / (radius * radius)
+    terms = (log_open - inverse * (u * u + v * v), 2.0 * inverse * u, 2.0 * inverse * v, -inverse)
+    values = [piece for term in terms for piece in pieces(term)]
+    values += [jnp.zeros((views, 2 * length), F32)] * (lines - len(values))
+    for block in range(2 * length // 128):
+        lanes = slice(128 * block, 128 * (block + 1))
+        for index, value in enumerate(values):
+            row_ref[block, pl.ds(index, views, stride=lines), :] = value[:, lanes]
+        for view in range(views):
+            terms_ref[view, :, lanes] = row_ref[block, lines * view : lines * (view + 1), :].astype(BF16)
 
 
 def shift_rows(value, by, fill, index):
@@ -445,10 +459,6 @@
     channels, length = features.shape
     tiles = tile_lists.shape[2]
     views = camera.shape[0]
-    column = lax.axis_index("cam")
-    tile_row = lax.axis_index("space")
-    image_width = TS * lax.axis_size("cam")
-    image_height = TS * lax.axis_size("space")
     shape = jax.ShapeDtypeStruct
 
     coded = pl.pallas_call(
@@ -465,30 +475,21 @@
     upper_slab = shifted(own_slab, "space", 1)
 
     packed = pack(decoder, targets[0, 0])
-    packed, upper_slab = lax.optimization_barrier((packed, upper_slab))
     received = lax.all_to_all(packed, "cam", 0, 0, tiled=True)
 
-    place = jnp.stack(
-        [
-            0.5 * image_width - (column * TS + 0.5 * TS),
-            0.5 * image_height - (tile_row * TS + 0.5 * TS),
-            tile_row,
-        ]
-    ).astype(F32)
     feature_bf, terms = pl.pallas_call(
         prep_kernel,
         out_shape=(shape((channels, 2 * length), BF16), shape((views, 16, 2 * length), BF16)),
         in_specs=[
             pl.BlockSpec(memory_space=pltpu.SMEM),
-            pl.BlockSpec(memory_space=pltpu.SMEM),
             whole(),
             whole(),
         ],
         out_specs=(whole(), whole()),
-        scratch_shapes=[pltpu.VMEM((16, 2 * length), F32)],
+        scratch_shapes=[pltpu.VMEM((2 * length // 128, views * 16, 128), F32)],
         cost_estimate=pl.CostEstimate(flops=10000000, bytes_accessed=1000000, transcendentals=20000),
         name="prep",
-    )(camera, place, own_slab, upper_slab)
+    )(camera.T, own_slab, upper_slab)
 
     saved = forward(codes, terms, feature_bf, decoder)
     own_sum, upper_sum = backward(received, codes, saved)

time: 66.2 us -> 63.6 us (0.961)
  starting transfers between devices: 25.2 us -> 18.9 us
  waiting for transfers between devices: 9.52 us -> 14.8 us
  other arithmetic: 1.51 us -> 0.01 us
    ppermute x2, waiting for transfers between devices: 8.03 us -> 13 us  [shifted(): return lax.ppermute(shard, axis, pairs)]
    ppermute x2, starting transfers between devices: 8.58 us -> 4.08 us  [shifted(): return lax.ppermute(shard, axis, pairs)]
    all_to_all x1, waiting for transfers between devices: 0.01 us -> 1.81 us  [on_device(): codes = lax.all_to_all(coded, 'cam', 0, 0, tiled=True)]
    all_to_all x1, starting transfers between devices: 8.13 us -> 6.35 us  [on_device(): received = lax.all_to_all(packed, 'cam', 0, 0, tiled=True)]
    all_to_all x1, waiting for transfers between devices: 1.49 us -> 0.01 us  [on_device(): received = lax.all_to_all(packed, 'cam', 0, 0, tiled=True)]
    concatenate x1, other arithmetic: 0.9 us -> 0.01 us  [on_device(): jnp.concatenate([features, positions, spreads[None], logits[None]], axis=0)]
    unnamed x19 -> x22, local copies, waits for them, and re-layouts: 3.83 us -> 3.77 us
  transfers between devices with their start and end apart: 4 -> 4, of which waited for: 3 -> 3; matrix products, arithmetic and copies ran while one was open for 3% -> 0% of each run, Pallas kernels for 24% -> 25%
where the time goes in v4:
time: 63.6 us; the launch traced here: 63 us
  Pallas kernels  24.8 us (39%)
  starting transfers between devices  18.9 us (30%)
  waiting for transfers between devices  14.8 us (23%)
  local copies, waits for them, and re-layouts  3.77 us (6%)
  between operations  0.75 us (1%)
    ppermute x2, waiting for transfers between devices, shifted(): return lax.ppermute(shard, axis, pairs)  13 us
    pallas_call x1, Pallas kernels, forward(): pl.pallas_call(forward_kernel, out_shape=tuple((shape((views,) + size, ki...  8.5 us
    all_to_all x1, starting transfers between devices, on_device(): codes = lax.all_to_all(coded, 'cam', 0, 0, tiled=True)  8.47 us
    pallas_call x1, Pallas kernels, backward(): pl.pallas_call(backward_kernel, out_shape=(shape((channels + 8, length),...  7.33 us
    all_to_all x1, starting transfers between devices, on_device(): received = lax.all_to_all(packed, 'cam', 0, 0, tiled=True)  6.35 us
    pallas_call x1, Pallas kernels, pack(): pl.pallas_call(pack_kernel, out_shape=jax.ShapeDtypeStruct(shape, jnp.int...  5.01 us
    ppermute x2, starting transfers between devices, shifted(): return lax.ppermute(shard, axis, pairs)  4.08 us
    unnamed x22, local copies, waits for them, and re-layouts  3.77 us
  transfers between devices with their start and end apart: 4, of which 3 were waited for; matrix products, arithmetic and copies ran while one was open for 0% of the time, Pallas kernels for 25%

profile of v4, /device:TPU:14, one launch (start us, length us, event | category | flops | bytes accessed | tf_op | source)
XLA Modules:
  0.0 63.0 jit_solution(2846286689435610612)
XLA Ops:
  0.6 0.0 copy-start.2
  0.6 0.0 copy-start.10
  0.7 0.0 copy-start.1
  0.7 0.7 %copy-done.1 = s32[1,1,16,256]{3,2,1,0:T(8,128)S(1)} copy-done((s32[1,1,16,256]{3,2,1,0:T(8,128)S(1)}, s32[1,1,16,256]{3,2,1,0:T(8,128)}, u32[]{:S(2)}) %copy-start.1) | copy-done | bytes 16408
  1.4 0.0 copy-start.3
  1.4 0.7 %copy-done.3 = s32[1,1,16]{2,1,0:T(1,128)S(1)} copy-done((s32[1,1,16]{2,1,0:T(1,128)S(1)}, s32[1,1,16]{2,1,0:T(1,128)}, u32[]{:S(2)}) %copy-start.3) | copy-done | bytes 88
  2.0 0.0 copy-start.8
  2.0 1.3 %lists.1 = s16[16,8,256]{2,1,0:T(8,128)(2,1)} custom-call(s32[16,256]{1,0:T(8,128)S(1)} %bitcast.7, s32[16]{0:T(128)S(1)} %bitcast.10), custom_call_target="tpu_custom_call" | custom-call | flops 1000000 | bytes 100000 | tf_op jit(solution)/shard_map/lists/pallas_call | solution.py:464
  3.4 8.5 %all-to-all-start = ((s16[16,8,256]{2,1,0:T(8,128)(2,1)}), s16[16,8,256]{2,1,0:T(8,128)(2,1)S(1)}, u32[]{:S(2)}, u32[]{:S(2)}) async-start(s16[16,8,256]{2,1,0:T(8,128)(2,1)} %lists.1), calls=%async_computation | async-start | bytes 131072 | tf_op jit(solution)/shard_map/all_to_all | solution.py:473
  11.8 5.0 %pack.1 = s16[16,72,256]{2,1,0:T(8,128)(2,1)} custom-call(bf16[64,512]{1,0:T(8,128)(2,1)} %decoder_ref.3, bf16[16,256,512]{2,1,0:T(8,128)(2,1)} %bitcast.11), custom_call_target="tpu_custom_call" | custom-call | flops 268435456 | bytes 4718592 | tf_op jit(solution)/shard_map/pack/pallas_call | solution.py:438
  16.9 1.8 %all-to-all-done.codes_ref.refs_0_ = s16[16,8,256]{2,1,0:T(8,128)(2,1)S(1)} async-done(((s16[16,8,256]{2,1,0:T(8,128)(2,1)}), s16[16,8,256]{2,1,0:T(8,128)(2,1)S(1)}, u32[]{:S(2)}, u32[]{:S(2)}) %all-to-all-start) | async-done | bytes 65568 | tf_op jit(solution)/shard_map/all_to_all | solution.py:473
  18.7 6.4 %all-to-all-start.1 = ((s16[16,72,256]{2,1,0:T(8,128)(2,1)}), s16[16,72,256]{2,1,0:T(8,128)(2,1)S(1)}, u32[]{:S(2)}, u32[]{:S(2)}) async-start(s16[16,72,256]{2,1,0:T(8,128)(2,1)} %pack.1), calls=%async_computation.1 | async-start | bytes 1179648 | tf_op jit(solution)/shard_map/all_to_all | solution.py:478
  25.0 0.0 copy-done.2
  25.0 0.0 copy-done.10
  25.0 0.0 copy-done.8
  25.1 0.0 copy-done.9
  25.1 0.0 copy-start.5
  25.1 1.9 %collective-permute-start = (f32[69,256]{1,0:T(8,128)S(1)}, f32[69,256]{1,0:T(8,128)S(1)}, u32[]{:S(2)}, u32[]{:S(2)}) collective-permute-start(f32[69,256]{1,0:T(8,128)S(1)} %pad_maximum_fusion.own_ref), channel_id=1, source_target_pairs={{0,1},{1,2},{2,3},{3,4},{4,5},{5,6},{6,7},{7,8},{8,9},{9,10},{10,1... | collective-permute-start | bytes 211976 | tf_op jit(solution)/shard_map/ppermute | solution.py:25
  27.0 10.7 %collective-permute-done.upper_ref = f32[69,256]{1,0:T(8,128)S(1)} collective-permute-done((f32[69,256]{1,0:T(8,128)S(1)}, f32[69,256]{1,0:T(8,128)S(1)}, u32[]{:S(2)}, u32[]{:S(2)}) %collective-permute-start) | collective-permute-done | bytes 70688 | tf_op jit(solution)/shard_map/ppermute | solution.py:25
  37.8 0.0 copy-done.5
  37.8 0.6 copy-done.7
  38.4 1.9 %prep.1 = (bf16[64,512]{1,0:T(8,128)(2,1)}, bf16[16,16,512]{2,1,0:T(8,128)(2,1)}) custom-call(f32[3,16]{1,0:T(4,128)} %bitcast.12, f32[69,256]{1,0:T(8,128)} %copy-done.5, f32[69,256]{1,0:T(8,128)} %copy-done.7), custom_call_target="tpu_custom_call" | custom-call | flops 10000000 | bytes 1000000 | tf_op jit(solution)/shard_map/prep/pallas_call | solution.py:480
  40.3 0.0 copy-done.6
  40.3 8.5 %forward.1 = (bf16[16,256,80]{2,1,0:T(8,128)(2,1)}, f32[16,256,256]{2,1,0:T(8,128)}, f32[16,256,256]{2,1,0:T(8,128)}, bf16[16,256,256]{2,1,0:T(8,128)(2,1)}, f32...) custom-call(s16[16,8,256]{2,1,0:T(8,128)(2,1)} %copy-done.6, bf16[16,16,512]{2,1,0:T(8,128)(2,1)} %get-tuple-element.14.terms_ref, ...), custom_call_target="tpu_custom_call" | custom-call | flops 1258291200 | bytes 11534336 | tf_op jit(solution)/shard_map/forward/pallas_call | solution.py:380
  48.8 0.0 all-to-all-done.1.refs_1_
  48.8 0.0 copy-start.4
  48.9 0.9 %copy-done.4 = s16[16,72,256]{2,1,0:T(8,128)(2,1)} copy-done((s16[16,72,256]{2,1,0:T(8,128)(2,1)}, s16[16,72,256]{2,1,0:T(8,128)(2,1)S(1)}, u32[]{:S(2)}) %copy-start.4) | copy-done | bytes 589848
  49.7 7.3 %backward.1 = (f32[72,256]{1,0:T(8,128)}, f32[72,256]{1,0:T(8,128)}) custom-call(s16[16,8,256]{2,1,0:T(8,128)(2,1)} %copy-done.6, s16[16,72,256]{2,1,0:T(8,128)(2,1)} %copy-done.4, f32[16,64,256]{2,1,0:T(8,128)} %get-tuple-element.16.refs_2_, bf16[16,256,80]{2,1,0:T(8,128)(2,1)} %get-tuple-element.17.refs_3_, f32[16,256,256]{2,1,0:T(8,128)} %get-tuple-element.18.refs_4_, ...), custom_call_target="tpu_custom_call" | custom-call | flops 1258291200 | bytes 11534336 | tf_op jit(solution)/shard_map/backward/pallas_call | solution.py:412
  57.1 2.2 %collective-permute-start.1 = (f32[72,256]{1,0:T(8,128)}, f32[72,256]{1,0:T(8,128)S(1)}, u32[]{:S(2)}, u32[]{:S(2)}) collective-permute-start(f32[72,256]{1,0:T(8,128)} %get-tuple-element.23), channel_id=1, source_target_pairs={{1,0},{2,1},{3,2},{4,3},{5,4},{6,5},{7,6},{8,7},{9,8},{10,9},{11,1... | collective-permute-start | bytes 221192 | tf_op jit(solution)/shard_map/ppermute | solution.py:25
  59.2 2.3 %collective-permute-done.1.returned_ref = f32[72,256]{1,0:T(8,128)S(1)} collective-permute-done((f32[72,256]{1,0:T(8,128)}, f32[72,256]{1,0:T(8,128)S(1)}, u32[]{:S(2)}, u32[]{:S(2)}) %collective-permute-start.1) | collective-permute-done | bytes 73760 | tf_op jit(solution)/shard_map/ppermute | solution.py:25
  61.5 0.9 %copy-done = f32[72,256]{1,0:T(8,128)S(1)} copy-done((f32[72,256]{1,0:T(8,128)S(1)}, f32[72,256]{1,0:T(8,128)}, u32[]{:S(2)}) %copy-start) | copy-done | bytes 73752
  62.4 0.6 %finish.1 = (f32[64,256]{1,0:T(8,128)}, f32[1,256]{1,0:T(1,128)}) custom-call(f32[72,256]{1,0:T(8,128)S(1)} %copy-done, f32[72,256]{1,0:T(8,128)S(1)} %collective-permute-done.1.returned_ref, f32[1,256]{1,0:T(1,128)S(1)} %bitcast.9), custom_call_target="tpu_custom_call" | custom-call | tf_op jit(solution)/shard_map/finish/pallas_call | solution.py:497
  (5 shorter events, 0.0 us)
Async XLA Ops:
  0.6 24.4 %copy-start.2 = (f32[256]{0:T(256)S(1)}, f32[256]{0:T(256)}, u32[]{:S(2)}) copy-start(f32[256]{0:T(256)} %param.12) | copy-start | bytes 3076
  0.6 24.4 %copy-start.10 = (f32[256]{0:T(256)S(1)}, f32[256]{0:T(256)}, u32[]{:S(2)}) copy-start(f32[256]{0:T(256)} %param.11) | copy-start | bytes 3076
  0.7 0.7 %copy-start.1 = (s32[1,1,16,256]{3,2,1,0:T(8,128)S(1)}, s32[1,1,16,256]{3,2,1,0:T(8,128)}, u32[]{:S(2)}) copy-start(s32[1,1,16,256]{3,2,1,0:T(8,128)} %param.15) | copy-start | bytes 49156
  1.4 0.7 %copy-start.3 = (s32[1,1,16]{2,1,0:T(1,128)S(1)}, s32[1,1,16]{2,1,0:T(1,128)}, u32[]{:S(2)}) copy-start(s32[1,1,16]{2,1,0:T(1,128)} %param.16) | copy-start | bytes 196
  2.0 23.0 %copy-start.8 = (f32[64,256]{1,0:T(8,128)S(1)}, f32[64,256]{1,0:T(8,128)}, u32[]{:S(2)}) copy-start(f32[64,256]{1,0:T(8,128)} %param.9) | copy-start | bytes 196612
  2.0 23.0 %copy-start.9 = (f32[3,256]{1,0:T(4,128)S(1)}, f32[3,256]{1,0:T(4,128)}, u32[]{:S(2)}) copy-start(f32[3,256]{1,0:T(4,128)} %param.10) | copy-start | bytes 9220
  3.4 15.3 %all-to-all-start = ((s16[16,8,256]{2,1,0:T(8,128)(2,1)}), s16[16,8,256]{2,1,0:T(8,128)(2,1)S(1)}, u32[]{:S(2)}, u32[]{:S(2)}) async-start(s16[16,8,256]{2,1,0:T(8,128)(2,1)} %lists.1), calls=%async_computation | async-start | bytes 131072 | tf_op jit(solution)/shard_map/all_to_all | solution.py:473
  18.7 21.7 %copy-start.6 = (s16[16,8,256]{2,1,0:T(8,128)(2,1)}, s16[16,8,256]{2,1,0:T(8,128)(2,1)S(1)}, u32[]{:S(2)}) copy-start(s16[16,8,256]{2,1,0:T(8,128)(2,1)S(1)} %all-to-all-done.codes_ref.refs_0_) | copy-start | bytes 196612
  18.7 30.2 %all-to-all-start.1 = ((s16[16,72,256]{2,1,0:T(8,128)(2,1)}), s16[16,72,256]{2,1,0:T(8,128)(2,1)S(1)}, u32[]{:S(2)}, u32[]{:S(2)}) async-start(s16[16,72,256]{2,1,0:T(8,128)(2,1)} %pack.1), calls=%async_computation.1 | async-start | bytes 1179648 | tf_op jit(solution)/shard_map/all_to_all | solution.py:478
  25.1 12.7 %copy-start.5 = (f32[69,256]{1,0:T(8,128)}, f32[69,256]{1,0:T(8,128)S(1)}, u32[]{:S(2)}) copy-start(f32[69,256]{1,0:T(8,128)S(1)} %pad_maximum_fusion.own_ref) | copy-start | bytes 211972
  25.1 12.7 %collective-permute-start = (f32[69,256]{1,0:T(8,128)S(1)}, f32[69,256]{1,0:T(8,128)S(1)}, u32[]{:S(2)}, u32[]{:S(2)}) collective-permute-start(f32[69,256]{1,0:T(8,128)S(1)} %pad_maximum_fusion.own_ref), channel_id=1, source_target_pairs={{0,1},{1,2},{2,3},{3,4},{4,5},{5,6},{6,7},{7,8},{8,9},{9,10},{10,1... | collective-permute-start | bytes 211976 | tf_op jit(solution)/shard_map/ppermute | solution.py:25
  37.8 0.6 copy-start.7
  48.8 0.9 %copy-start.4 = (s16[16,72,256]{2,1,0:T(8,128)(2,1)}, s16[16,72,256]{2,1,0:T(8,128)(2,1)S(1)}, u32[]{:S(2)}) copy-start(s16[16,72,256]{2,1,0:T(8,128)(2,1)S(1)} %all-to-all-done.1.refs_1_) | copy-start | bytes 1769476
  57.1 4.4 %collective-permute-start.1 = (f32[72,256]{1,0:T(8,128)}, f32[72,256]{1,0:T(8,128)S(1)}, u32[]{:S(2)}, u32[]{:S(2)}) collective-permute-start(f32[72,256]{1,0:T(8,128)} %get-tuple-element.23), channel_id=1, source_target_pairs={{1,0},{2,1},{3,2},{4,3},{5,4},{6,5},{7,6},{8,7},{9,8},{10,9},{11,1... | collective-permute-start | bytes 221192 | tf_op jit(solution)/shard_map/ppermute | solution.py:25
  61.5 0.9 %copy-start = (f32[72,256]{1,0:T(8,128)S(1)}, f32[72,256]{1,0:T(8,128)}, u32[]{:S(2)}) copy-start(f32[72,256]{1,0:T(8,128)} %get-tuple-element.22.own_ref) | copy-start | bytes 221188

commit v5 on v4

--- a/solution.py
+++ b/solution.py
@@ -89,7 +89,7 @@
         outgoing(turn).wait()
 
 
-def prep_kernel(camera_ref, own_ref, upper_ref, feature_ref, terms_ref, row_ref):
+def project(camera_ref, own_ref, upper_ref, feature_ref, terms_ref, row_ref):
     channels, length = feature_ref.shape[0], own_ref.shape[1]
     views, lines = terms_ref.shape[0], terms_ref.shape[1]
     column = lax.axis_index("cam").astype(F32)
@@ -210,34 +210,61 @@
     projected_ref[...] = dot(squares_ref[...], jnp.concatenate([composite] * 3, axis=0), NN)
 
 
-def forward_kernel(
-    codes_ref, terms_ref, feature_ref, decoder_ref,
-    entry_ref, a_ref, w_ref, wb_ref, ends_ref, projected_ref,
-    squares_ref, basis_ref, wanted_ref, hot_ref
-):
+def forward_kernel(codes_ref, camera_ref, block_ref, upper_ref, decoder_ref, *refs):
+    count = (len(refs) - 8) // 2
+    outs, held = refs[:count], refs[count : 2 * count]
+    feature_ref, terms_ref, row_ref, squares_ref, basis_ref, wanted_ref, hot_ref, sem = refs[2 * count :]
     channels = feature_ref.shape[0]
-
-    @pl.when(pl.program_id(0) == 0)
-    def _():
-        set_wanted(wanted_ref)
-        for turn, piece in enumerate(pieces(dot(decoder_ref[...], decoder_ref[...], NT))):
-            squares_ref[:, channels * turn : channels * (turn + 1)] = piece.astype(BF16)
-        line = lax.broadcasted_iota(jnp.int32, basis_ref.shape, 0) - channels
-        pixel = lax.broadcasted_iota(jnp.int32, basis_ref.shape, 1)
-        px = (pixel % TS).astype(F32) - (0.5 * TS - 0.5)
-        py = (pixel // TS).astype(F32) - (0.5 * TS - 0.5)
-        basis = jnp.where(line < 3, 1.0, jnp.where(line < 6, px, jnp.where(line < 9, py, px * px + py * py)))
-        basis = jnp.where(line == 12, 1.0, basis)
-        basis_ref[...] = jnp.where((line < 0) | (line > 12), 0.0, basis).astype(BF16)
-
-    in_turns(
-        forward_tile(
-            codes_ref.at[turn], terms_ref.at[turn],
-            feature_ref, squares_ref, basis_ref, wanted_ref,
-            *(ref.at[turn] for ref in (entry_ref, a_ref, w_ref, wb_ref, ends_ref, projected_ref, hot_ref)),
+    group, turns = hot_ref.shape[0], sem.shape[0]
+    project(camera_ref, block_ref, upper_ref, feature_ref, terms_ref, row_ref)
+    set_wanted(wanted_ref)
+    for turn, piece in enumerate(pieces(dot(decoder_ref[...], decoder_ref[...], NT))):
+        squares_ref[:, channels * turn : channels * (turn + 1)] = piece.astype(BF16)
+    line = lax.broadcasted_iota(jnp.int32, basis_ref.shape, 0) - channels
+    pixel = lax.broadcasted_iota(jnp.int32, basis_ref.shape, 1)
+    px = (pixel % TS).astype(F32) - (0.5 * TS - 0.5)
+    py = (pixel // TS).astype(F32) - (0.5 * TS - 0.5)
+    basis = jnp.where(line < 3, 1.0, jnp.where(line < 6, px, jnp.where(line < 9, py, px * px + py * py)))
+    basis = jnp.where(line == 12, 1.0, basis)
+    basis_ref[...] = jnp.where((line < 0) | (line > 12), 0.0, basis).astype(BF16)
+
+    def copies(turn, first, last):
+        span = pl.ds(turn * group, group)
+        return [
+            pltpu.make_async_copy(held[index].at[span], outs[index].at[span], sem.at[turn, index])
+            for index in range(first, last)
+        ]
+
+    def build(turn, carry):
+        def leaving(first, last):
+            def start():
+                for copy in copies(turn, first, last):
+                    copy.start()
+
+            return start
+
+        def nothing():
+            pass
+
+        tile = turn * group
+        in_turns(
+            (
+                forward_tile(
+                    codes_ref.at[tile + step], terms_ref.at[tile + step],
+                    feature_ref, squares_ref, basis_ref, wanted_ref,
+                    *(ref.at[tile + step] for ref in held), hot_ref.at[step],
+                )
+                for step in range(group)
+            ),
+            (nothing, nothing, nothing, leaving(0, 2), nothing, leaving(2, count - 1)),
         )
-        for turn in range(hot_ref.shape[0])
-    )
+        leaving(count - 1, count)()
+        return carry
+
+    lax.fori_loop(0, turns, build, 0)
+    for turn in range(turns):
+        for copy in copies(turn, 0, count):
+            copy.wait()
 
 
 def backward_tile(
@@ -353,14 +380,6 @@
     return pltpu.CompilerParams(vmem_limit_bytes=8 << 20)
 
 
-def blocks(group, *shape):
-    return pl.BlockSpec((group,) + shape, lambda t: (t,) + (0,) * len(shape))
-
-
-def fixed(*shape):
-    return pl.BlockSpec(shape, lambda t: (0,) * len(shape))
-
-
 def kept_sizes(channels, length):
     return (
         ((length, channels + 16), BF16),
@@ -372,27 +391,26 @@
     )
 
 
-def forward(codes, terms, feature_bf, decoder, group=4):
+def forward(codes, camera_t, own_slab, upper_slab, decoder, group=4):
     channels, decoded = decoder.shape
     views, length = codes.shape[0], codes.shape[2]
     shape = jax.ShapeDtypeStruct
-    kept = kept_sizes(channels, length)
+    kept = [shape((views,) + size, kind) for size, kind in kept_sizes(channels, length)]
     return pl.pallas_call(
         forward_kernel,
-        out_shape=tuple(shape((views,) + size, kind) for size, kind in kept),
-        grid=(views // group,),
-        in_specs=[
-            blocks(group, 8, length),
-            blocks(group, 16, 2 * length),
-            fixed(channels, 2 * length),
-            fixed(channels, decoded),
-        ],
-        out_specs=tuple(blocks(group, *size) for size, _ in kept),
+        out_shape=tuple(kept),
+        in_specs=[whole(), pl.BlockSpec(memory_space=pltpu.SMEM), whole(), whole(), whole()],
+        out_specs=(pl.BlockSpec(memory_space=pl.ANY),) * len(kept),
         scratch_shapes=[
+            *(pltpu.VMEM(out.shape, out.dtype) for out in kept),
+            pltpu.VMEM((channels, 2 * length), BF16),
+            pltpu.VMEM((views, 16, 2 * length), BF16),
+            pltpu.VMEM((2 * length // 128, views * 16, 128), F32),
             pltpu.VMEM((channels, 3 * channels), BF16),
             pltpu.VMEM((channels + 16, length), BF16),
             pltpu.VMEM((2 * length, 128), BF16),
             pltpu.VMEM((group, 2 * length, length), BF16),
+            pltpu.SemaphoreType.DMA((views // group, len(kept))),
         ],
         cost_estimate=pl.CostEstimate(
             flops=views * 2 * length * length * 600,
@@ -400,7 +418,7 @@
             transcendentals=views * length * length,
         ),
         name="forward",
-    )(codes, terms, feature_bf, decoder)
+    )(codes, camera_t, own_slab, upper_slab, decoder)
 
 
 def backward(received, codes, saved, group=4):
@@ -458,7 +476,6 @@
 def on_device(features, positions, spreads, logits, camera, decoder, tile_lists, counts, targets):
     channels, length = features.shape
     tiles = tile_lists.shape[2]
-    views = camera.shape[0]
     shape = jax.ShapeDtypeStruct
 
     coded = pl.pallas_call(
@@ -466,7 +483,6 @@
         out_shape=shape((tiles, 8, length), jnp.int16),
         in_specs=[whole(), pl.BlockSpec(memory_space=pltpu.SMEM)],
         out_specs=whole(),
-        compiler_params=small(),
         cost_estimate=pl.CostEstimate(flops=1000000, bytes_accessed=100000, transcendentals=0),
         name="lists",
     )(tile_lists[0, 0], counts[0, 0])
@@ -477,21 +493,7 @@
     packed = pack(decoder, targets[0, 0])
     received = lax.all_to_all(packed, "cam", 0, 0, tiled=True)
 
-    feature_bf, terms = pl.pallas_call(
-        prep_kernel,
-        out_shape=(shape((channels, 2 * length), BF16), shape((views, 16, 2 * length), BF16)),
-        in_specs=[
-            pl.BlockSpec(memory_space=pltpu.SMEM),
-            whole(),
-            whole(),
-        ],
-        out_specs=(whole(), whole()),
-        scratch_shapes=[pltpu.VMEM((2 * length // 128, views * 16, 128), F32)],
-        cost_estimate=pl.CostEstimate(flops=10000000, bytes_accessed=1000000, transcendentals=20000),
-        name="prep",
-    )(camera.T, own_slab, upper_slab)
-
-    saved = forward(codes, terms, feature_bf, decoder)
+    saved = forward(codes, camera.T, own_slab, upper_slab, decoder)
     own_sum, upper_sum = backward(received, codes, saved)
     returned = shifted(upper_sum, "space", -1)
     grad_features, grad_logits = pl.pallas_call(

time: 63.6 us -> 62.4 us (0.981)
  starting transfers between devices: 18.9 us -> 20.6 us
  Pallas kernels: 24.8 us -> 23.3 us
  local copies, waits for them, and re-layouts: 3.77 us -> 2.4 us
    pallas_call x2 -> x1, Pallas kernels: 10.4 us -> 8.77 us  [forward(): pl.pallas_call(forward_kernel, out_shape=tuple(kept), in_specs=[whole(),...]
    ppermute x2, starting transfers between devices: 4.08 us -> 5.74 us  [shifted(): return lax.ppermute(shard, axis, pairs)]
    unnamed x22 -> x18, local copies, waits for them, and re-layouts: 3.77 us -> 2.4 us
  transfers between devices with their start and end apart: 4 -> 4, of which waited for: 3 -> 3; matrix products, arithmetic and copies ran while one was open for 0% -> 0% of each run, Pallas kernels for 25% -> 22%
where the time goes in v5:
time: 62.4 us; the launch traced here: 61.9 us
  Pallas kernels  23.3 us (37%)
  starting transfers between devices  20.6 us (33%)
  waiting for transfers between devices  14.8 us (24%)
  local copies, waits for them, and re-layouts  2.4 us (4%)
  between operations  0.77 us (1%)
    ppermute x2, waiting for transfers between devices, shifted(): return lax.ppermute(shard, axis, pairs)  13 us
    pallas_call x1, Pallas kernels, forward(): pl.pallas_call(forward_kernel, out_shape=tuple(kept), in_specs=[whole(),...  8.77 us
    all_to_all x1, starting transfers between devices, on_device(): codes = lax.all_to_all(coded, 'cam', 0, 0, tiled=True)  8.47 us
    pallas_call x1, Pallas kernels, backward(): pl.pallas_call(backward_kernel, out_shape=(shape((channels + 8, length),...  7.33 us
    all_to_all x1, starting transfers between devices, on_device(): received = lax.all_to_all(packed, 'cam', 0, 0, tiled=True)  6.35 us
    ppermute x2, starting transfers between devices, shifted(): return lax.ppermute(shard, axis, pairs)  5.74 us
    pallas_call x1, Pallas kernels, pack(): pl.pallas_call(pack_kernel, out_shape=jax.ShapeDtypeStruct(shape, jnp.int...  5 us
    unnamed x18, local copies, waits for them, and re-layouts  2.4 us
  transfers between devices with their start and end apart: 4, of which 3 were waited for; matrix products, arithmetic and copies ran while one was open for 0% of the time, Pallas kernels for 22%

profile of v5, /device:TPU:14, one launch (start us, length us, event | category | flops | bytes accessed | tf_op | source)
XLA Modules:
  0.0 61.9 jit_solution(2932245252855172131)
XLA Ops:
  0.6 0.0 copy-start.1
  0.6 0.0 copy-start.7
  0.7 0.0 copy-start.6
  0.7 0.0 copy-start.5
  0.7 1.6 %lists.1 = s16[16,8,256]{2,1,0:T(8,128)(2,1)} custom-call(s32[16,256]{1,0:T(8,128)} %bitcast.10, s32[16]{0:T(128)} %bitcast.12), custom_call_target="tpu_custom_call" | custom-call | flops 1000000 | bytes 100000 | tf_op jit(solution)/shard_map/lists/pallas_call | solution.py:481
  2.3 8.5 %all-to-all-start = ((s16[16,8,256]{2,1,0:T(8,128)(2,1)}), s16[16,8,256]{2,1,0:T(8,128)(2,1)S(1)}, u32[]{:S(2)}, u32[]{:S(2)}) async-start(s16[16,8,256]{2,1,0:T(8,128)(2,1)} %lists.1), calls=%async_computation | async-start | bytes 131072 | tf_op jit(solution)/shard_map/all_to_all | solution.py:489
  10.7 5.0 %pack.1 = s16[16,72,256]{2,1,0:T(8,128)(2,1)} custom-call(bf16[64,512]{1,0:T(8,128)(2,1)} %decoder_ref.3, bf16[16,256,512]{2,1,0:T(8,128)(2,1)} %bitcast.9), custom_call_target="tpu_custom_call" | custom-call | flops 268435456 | bytes 4718592 | tf_op jit(solution)/shard_map/pack/pallas_call | solution.py:456
  15.7 1.8 %all-to-all-done.codes_ref.refs_0_ = s16[16,8,256]{2,1,0:T(8,128)(2,1)S(1)} async-done(((s16[16,8,256]{2,1,0:T(8,128)(2,1)}), s16[16,8,256]{2,1,0:T(8,128)(2,1)S(1)}, u32[]{:S(2)}, u32[]{:S(2)}) %all-to-all-start) | async-done | bytes 65568 | tf_op jit(solution)/shard_map/all_to_all | solution.py:489
  17.6 0.0 copy-start.3
  17.6 6.3 %all-to-all-start.1 = ((s16[16,72,256]{2,1,0:T(8,128)(2,1)}), s16[16,72,256]{2,1,0:T(8,128)(2,1)S(1)}, u32[]{:S(2)}, u32[]{:S(2)}) async-start(s16[16,72,256]{2,1,0:T(8,128)(2,1)} %pack.1), calls=%async_computation.1 | async-start | bytes 1179648 | tf_op jit(solution)/shard_map/all_to_all | solution.py:494
  23.9 0.0 copy-done.1
  23.9 0.0 copy-done.7
  23.9 0.0 copy-done.6
  23.9 0.0 copy-done.5
  24.0 0.0 copy-start.4
  24.0 1.9 %collective-permute-start = (f32[69,256]{1,0:T(8,128)S(1)}, f32[69,256]{1,0:T(8,128)S(1)}, u32[]{:S(2)}, u32[]{:S(2)}) collective-permute-start(f32[69,256]{1,0:T(8,128)S(1)} %pad_maximum_fusion.block_ref), channel_id=1, source_target_pairs={{0,1},{1,2},{2,3},{3,4},{4,5},{5,6},{6,7},{7,8},{8,9},{9,10},{10,1... | collective-permute-start | bytes 211976 | tf_op jit(solution)/shard_map/ppermute | solution.py:25
  25.9 10.7 %collective-permute-done.upper_ref = f32[69,256]{1,0:T(8,128)S(1)} collective-permute-done((f32[69,256]{1,0:T(8,128)S(1)}, f32[69,256]{1,0:T(8,128)S(1)}, u32[]{:S(2)}, u32[]{:S(2)}) %collective-permute-start) | collective-permute-done | bytes 70688 | tf_op jit(solution)/shard_map/ppermute | solution.py:25
  36.7 0.0 copy-start.8
  36.7 0.0 copy-done.3
  36.7 0.0 copy-done.4
  36.7 0.6 %copy-done.8 = f32[69,256]{1,0:T(8,128)} copy-done((f32[69,256]{1,0:T(8,128)}, f32[69,256]{1,0:T(8,128)S(1)}, u32[]{:S(2)}) %copy-start.8) | copy-done | bytes 70680
  37.3 8.8 %forward.1 = (bf16[16,256,80]{2,1,0:T(8,128)(2,1)}, f32[16,256,256]{2,1,0:T(8,128)}, f32[16,256,256]{2,1,0:T(8,128)}, bf16[16,256,256]{2,1,0:T(8,128)(2,1)}, f32...) custom-call(s16[16,8,256]{2,1,0:T(8,128)(2,1)} %copy-done.3, f32[3,16]{1,0:T(4,128)} %bitcast.13, f32[69,256]{1,0:T(8,128)} %copy-done.4, ...), custom_call_target="tpu_custom_call" | custom-call | flops 1258291200 | bytes 11534336 | tf_op jit(solution)/shard_map/forward/pallas_call | solution.py:399
  46.1 0.0 all-to-all-done.1.refs_1_
  46.1 0.0 copy-start.2
  46.1 0.9 %copy-done.2 = s16[16,72,256]{2,1,0:T(8,128)(2,1)} copy-done((s16[16,72,256]{2,1,0:T(8,128)(2,1)}, s16[16,72,256]{2,1,0:T(8,128)(2,1)S(1)}, u32[]{:S(2)}) %copy-start.2) | copy-done | bytes 589848
  47.0 7.3 %backward.1 = (f32[72,256]{1,0:T(8,128)}, f32[72,256]{1,0:T(8,128)}) custom-call(s16[16,8,256]{2,1,0:T(8,128)(2,1)} %copy-done.3, s16[16,72,256]{2,1,0:T(8,128)(2,1)} %copy-done.2, f32[16,64,256]{2,1,0:T(8,128)} %get-tuple-element.12.refs_2_, bf16[16,256,80]{2,1,0:T(8,128)(2,1)} %get-tuple-element.13.refs_3_, f32[16,256,256]{2,1,0:T(8,128)} %get-tuple-element.14.refs_4_, ...), custom_call_target="tpu_custom_call" | custom-call | flops 1258291200 | bytes 11534336 | tf_op jit(solution)/shard_map/backward/pallas_call | solution.py:430
  54.3 3.8 %collective-permute-start.1 = (f32[72,256]{1,0:T(8,128)}, f32[72,256]{1,0:T(8,128)S(1)}, u32[]{:S(2)}, u32[]{:S(2)}) collective-permute-start(f32[72,256]{1,0:T(8,128)} %get-tuple-element.19), channel_id=1, source_target_pairs={{1,0},{2,1},{3,2},{4,3},{5,4},{6,5},{7,6},{8,7},{9,8},{10,9},{11,1... | collective-permute-start | bytes 221192 | tf_op jit(solution)/shard_map/ppermute | solution.py:25
  58.1 2.3 %collective-permute-done.1.returned_ref = f32[72,256]{1,0:T(8,128)S(1)} collective-permute-done((f32[72,256]{1,0:T(8,128)}, f32[72,256]{1,0:T(8,128)S(1)}, u32[]{:S(2)}, u32[]{:S(2)}) %collective-permute-start.1) | collective-permute-done | bytes 73760 | tf_op jit(solution)/shard_map/ppermute | solution.py:25
  60.4 0.0 copy-start
  60.4 0.9 %copy-done = f32[72,256]{1,0:T(8,128)S(1)} copy-done((f32[72,256]{1,0:T(8,128)S(1)}, f32[72,256]{1,0:T(8,128)}, u32[]{:S(2)}) %copy-start) | copy-done | bytes 73752
  61.3 0.6 %finish.1 = (f32[64,256]{1,0:T(8,128)}, f32[1,256]{1,0:T(1,128)}) custom-call(f32[72,256]{1,0:T(8,128)S(1)} %copy-done, f32[72,256]{1,0:T(8,128)S(1)} %collective-permute-done.1.returned_ref, f32[1,256]{1,0:T(1,128)S(1)} %bitcast.8), custom_call_target="tpu_custom_call" | custom-call | tf_op jit(solution)/shard_map/finish/pallas_call | solution.py:499
  (1 shorter events, 0.0 us)
Async XLA Ops:
  0.6 23.3 %copy-start.1 = (f32[256]{0:T(256)S(1)}, f32[256]{0:T(256)}, u32[]{:S(2)}) copy-start(f32[256]{0:T(256)} %param.12) | copy-start | bytes 3076
  0.6 23.3 %copy-start.7 = (f32[256]{0:T(256)S(1)}, f32[256]{0:T(256)}, u32[]{:S(2)}) copy-start(f32[256]{0:T(256)} %param.11) | copy-start | bytes 3076
  0.7 23.3 %copy-start.6 = (f32[3,256]{1,0:T(4,128)S(1)}, f32[3,256]{1,0:T(4,128)}, u32[]{:S(2)}) copy-start(f32[3,256]{1,0:T(4,128)} %param.10) | copy-start | bytes 9220
  0.7 23.3 %copy-start.5 = (f32[64,256]{1,0:T(8,128)S(1)}, f32[64,256]{1,0:T(8,128)}, u32[]{:S(2)}) copy-start(f32[64,256]{1,0:T(8,128)} %param.9) | copy-start | bytes 196612
  2.3 15.3 %all-to-all-start = ((s16[16,8,256]{2,1,0:T(8,128)(2,1)}), s16[16,8,256]{2,1,0:T(8,128)(2,1)S(1)}, u32[]{:S(2)}, u32[]{:S(2)}) async-start(s16[16,8,256]{2,1,0:T(8,128)(2,1)} %lists.1), calls=%async_computation | async-start | bytes 131072 | tf_op jit(solution)/shard_map/all_to_all | solution.py:489
  17.6 19.1 %copy-start.3 = (s16[16,8,256]{2,1,0:T(8,128)(2,1)}, s16[16,8,256]{2,1,0:T(8,128)(2,1)S(1)}, u32[]{:S(2)}) copy-start(s16[16,8,256]{2,1,0:T(8,128)(2,1)S(1)} %all-to-all-done.codes_ref.refs_0_) | copy-start | bytes 196612
  17.6 28.5 %all-to-all-start.1 = ((s16[16,72,256]{2,1,0:T(8,128)(2,1)}), s16[16,72,256]{2,1,0:T(8,128)(2,1)S(1)}, u32[]{:S(2)}, u32[]{:S(2)}) async-start(s16[16,72,256]{2,1,0:T(8,128)(2,1)} %pack.1), calls=%async_computation.1 | async-start | bytes 1179648 | tf_op jit(solution)/shard_map/all_to_all | solution.py:494
  24.0 12.7 %copy-start.4 = (f32[69,256]{1,0:T(8,128)}, f32[69,256]{1,0:T(8,128)S(1)}, u32[]{:S(2)}) copy-start(f32[69,256]{1,0:T(8,128)S(1)} %pad_maximum_fusion.block_ref) | copy-start | bytes 211972
  24.0 12.7 %collective-permute-start = (f32[69,256]{1,0:T(8,128)S(1)}, f32[69,256]{1,0:T(8,128)S(1)}, u32[]{:S(2)}, u32[]{:S(2)}) collective-permute-start(f32[69,256]{1,0:T(8,128)S(1)} %pad_maximum_fusion.block_ref), channel_id=1, source_target_pairs={{0,1},{1,2},{2,3},{3,4},{4,5},{5,6},{6,7},{7,8},{8,9},{9,10},{10,1... | collective-permute-start | bytes 211976 | tf_op jit(solution)/shard_map/ppermute | solution.py:25
  36.7 0.6 %copy-start.8 = (f32[69,256]{1,0:T(8,128)}, f32[69,256]{1,0:T(8,128)S(1)}, u32[]{:S(2)}) copy-start(f32[69,256]{1,0:T(8,128)S(1)} %collective-permute-done.upper_ref) | copy-start | bytes 211972
  46.1 0.9 %copy-start.2 = (s16[16,72,256]{2,1,0:T(8,128)(2,1)}, s16[16,72,256]{2,1,0:T(8,128)(2,1)S(1)}, u32[]{:S(2)}) copy-start(s16[16,72,256]{2,1,0:T(8,128)(2,1)S(1)} %all-to-all-done.1.refs_1_) | copy-start | bytes 1769476
  54.3 6.1 %collective-permute-start.1 = (f32[72,256]{1,0:T(8,128)}, f32[72,256]{1,0:T(8,128)S(1)}, u32[]{:S(2)}, u32[]{:S(2)}) collective-permute-start(f32[72,256]{1,0:T(8,128)} %get-tuple-element.19), channel_id=1, source_target_pairs={{1,0},{2,1},{3,2},{4,3},{5,4},{6,5},{7,6},{8,7},{9,8},{10,9},{11,1... | collective-permute-start | bytes 221192 | tf_op jit(solution)/shard_map/ppermute | solution.py:25
  60.4 0.9 %copy-start = (f32[72,256]{1,0:T(8,128)S(1)}, f32[72,256]{1,0:T(8,128)}, u32[]{:S(2)}) copy-start(f32[72,256]{1,0:T(8,128)} %get-tuple-element.18.own_ref) | copy-start | bytes 221188
